TPU v7x, 32 devices: a whole 2x2x4 slice. The times are simulated.
32 devices in a mesh: patch: 16 (over z, y, core), chan: 2 (over x).
Axes of the slice: x: 2, y: 2, z: 4, core: 2. Of those that a mesh axis runs over, the one named last changes fastest.
Arguments:
- fields: bfloat16 [16, 128, 1024], P('patch', 'chan'), may hold values from -6 to 6
- w_one: bfloat16 [9, 512, 128], P(None, 'chan'), may hold values from -0.1875 to 0.1875
- bias_one: float32 [512], P('chan'), may hold values from -3 to 3
- w_two: bfloat16 [9, 128, 512], P(None, None, 'chan'), may hold values from -0.09375 to 0.09375
- neighbour: int32 [16, 4], replicated, may hold values from 0 to 15, as said below
- seam_code: int32 [16, 4], replicated, may hold values from 0 to 7, as said below
- band_order: int32 [16], replicated, may hold values from 0 to 15, each once
- target: bfloat16 [16, 128, 1024], P('patch', 'chan'), may hold values from -6 to 6
- lat_weight: bfloat16 [16, 1024], P('patch'), may hold values from 0.099609375 to 1
Outputs:
- loss_value: float32 [], replicated
- grad_one: float32 [9, 512, 128], P(None, 'chan')
- grad_two: float32 [9, 128, 512], P(None, None, 'chan')
- grad_bias: float32 [512], P('chan')
Inputs may be any that keep to these rules, and one draw needn't show every extreme that they name: The sides of all patches are paired: side s of patch p borders side t = seam_code[p, s] mod 4 of patch q = neighbour[p, s], and then neighbour[q, t] = p, seam_code[q, t] mod 4 = s, and both codes agree on being 4 or more; so every edge is read by exactly one side of one other patch, and the four sides of a patch face four different patches. `seam_code`: code mod 4 names the neighbour's edge that forms the seam; codes 4 and above run that edge reversed, alike on both sides of a seam. `band_order`: each patch fills exactly one slot of every band.
All inputs are finite; a program needn't handle non-finite values.
Results may differ from a plain program's by a relative error of at most 0.0021.
Values may be sent and summed in bfloat16 or wider, within the bound.
A program may use at most 64 MiB of HBM per device.

v0:
```python
import math

import jax
import jax.numpy as jnp
from jax import lax
from jax.sharding import PartitionSpec as P

C = 128
P_SIZE = 32


def edges_of(field):
    return jnp.stack(
        [field[..., 0, :], field[..., -1, :], field[..., :, 0], field[..., :, -1]], axis=-3
    )


def with_frame(field, strips):
    padded = jnp.pad(field, ((0, 0), (1, 1), (1, 1)))
    padded = padded.at[:, 0, 1:-1].set(strips[0])
    padded = padded.at[:, -1, 1:-1].set(strips[1])
    padded = padded.at[:, 1:-1, 0].set(strips[2])
    padded = padded.at[:, 1:-1, -1].set(strips[3])
    return padded


def tap_list(padded):
    length = padded.shape[-1] - 2
    span = length + 2
    flat = jnp.pad(padded.reshape(padded.shape[0], span * span), ((0, 0), (0, 2)))
    return [
        flat[:, row_off * span + col_off : row_off * span + col_off + length * span]
        for row_off in range(3)
        for col_off in range(3)
    ]


def narrow(wide, length):
    return wide.reshape(wide.shape[0], length, length + 2)[:, :, :length].reshape(
        wide.shape[0], length * length
    )


def widen(values, length):
    shaped = values.reshape(values.shape[0], length, length)
    return jnp.pad(shaped, ((0, 0), (0, 0), (0, 2))).reshape(values.shape[0], length * (length + 2))


def apply_taps(weight, taps):
    summed = jnp.zeros((weight.shape[1], taps[0].shape[1]), jnp.float32)
    for tap_index in range(9):
        summed = summed + jnp.dot(
            weight[tap_index], taps[tap_index], preferred_element_type=jnp.float32
        )
    return summed


def smooth_gate(values):
    return jax.nn.gelu(values, approximate=True)


def oriented(strips, codes):
    return jnp.where((codes >= 4)[:, None, None], strips[..., ::-1], strips)


def on_device(fields, w_one, bias_one, w_two, neighbour, seam_code, band_order, target, lat_weight):
    length = P_SIZE
    span = P_SIZE + 2
    cell_count = P_SIZE * P_SIZE
    patch_count = lax.axis_size("patch")
    part_len = cell_count // patch_count
    own_index = lax.axis_index("patch")
    own_nbr = lax.dynamic_slice_in_dim(neighbour, own_index, 1, 0)[0]
    own_code = lax.dynamic_slice_in_dim(seam_code, own_index, 1, 0)[0]
    sides = jnp.arange(4, dtype=jnp.int32)

    def pick_edges(shard_rows):
        row_ids = jnp.arange(shard_rows.shape[0], dtype=jnp.int32)
        chosen = (own_nbr[:, None, None] == row_ids[None, :, None]) & (
            (own_code % 4)[:, None, None] == sides[None, None, :]
        )
        return jnp.einsum(
            "srt,rtcq->scq",
            chosen.astype(shard_rows.dtype),
            shard_rows,
            preferred_element_type=jnp.float32,
        )

    local = fields[0]
    local_ch = local.shape[0]
    whole = lax.all_gather(local, "chan", axis=0, tiled=True)
    grid = whole.reshape(whole.shape[0], length, length)
    seams = pick_edges(lax.all_gather(edges_of(grid)[None], "patch", axis=0, tiled=True))
    x_pad = with_frame(grid, oriented(seams, own_code).astype(jnp.bfloat16))
    x_taps = tap_list(x_pad)
    preact = narrow(apply_taps(w_one, x_taps), length) + bias_one[:, None]
    hidden = smooth_gate(preact).astype(jnp.bfloat16)
    inner_ch = hidden.shape[0]
    hidden_grid = hidden.reshape(inner_ch, length, length)
    hidden_seams = pick_edges(
        lax.all_gather(edges_of(hidden_grid)[None], "patch", axis=0, tiled=True)
    )
    hidden_strips = oriented(hidden_seams, own_code).astype(jnp.bfloat16)
    h_pad = with_frame(hidden_grid, hidden_strips)
    h_taps = tap_list(h_pad)
    mixed = lax.psum_scatter(
        narrow(apply_taps(w_two, h_taps), length), "chan", scatter_dimension=0, tiled=True
    )
    outputs = local.astype(jnp.float32) + mixed
    inv_root = 1.0 / math.sqrt(patch_count * cell_count)
    inverse = (
        jnp.zeros((patch_count,), jnp.int32)
        .at[band_order]
        .set(jnp.arange(patch_count, dtype=jnp.int32))
    )
    arrived = lax.all_to_all(
        outputs.reshape(local_ch, patch_count, part_len),
        "patch",
        split_axis=1,
        concat_axis=1,
        tiled=True,
    )
    in_band = arrived[:, band_order, :].reshape(local_ch, cell_count)
    misfit = in_band - target[0].astype(jnp.float32)
    lat_w = lat_weight[0].astype(jnp.float32)[None, :]
    partial_loss = jnp.sum(lat_w * misfit * misfit)
    band_grad = (
        (lat_w * misfit * inv_root).astype(jnp.bfloat16).reshape(local_ch, patch_count, part_len)
    )
    returned = lax.all_to_all(
        band_grad[:, inverse, :], "patch", split_axis=1, concat_axis=1, tiled=True
    )
    grad_out = returned.reshape(local_ch, cell_count)
    loss_value = lax.psum(partial_loss, ("patch", "chan")) / (patch_count * cell_count * C)
    grad_full = lax.all_gather(grad_out, "chan", axis=0, tiled=True)
    grad_wide = widen(grad_full, length)
    flat_len = span * span + 2
    wide_len = length * span
    frame_flat = jnp.zeros((inner_ch, flat_len), jnp.float32)
    tap_index = 0
    for row_off in range(3):
        for col_off in range(3):
            block = lax.dot_general(
                w_two[tap_index],
                grad_wide,
                (((0,), (0,)), ((), ())),
                preferred_element_type=jnp.float32,
            )
            offset = row_off * span + col_off
            frame_flat = frame_flat + jnp.pad(
                block, ((0, 0), (offset, flat_len - offset - wide_len))
            )
            tap_index = tap_index + 1
    grad_frame = frame_flat[:, : span * span].reshape(inner_ch, span, span)
    interior = grad_frame[:, 1:-1, 1:-1]
    frames = jnp.stack(
        [
            grad_frame[:, 0, 1:-1],
            grad_frame[:, -1, 1:-1],
            grad_frame[:, 1:-1, 0],
            grad_frame[:, 1:-1, -1],
        ]
    )
    shard_rows = lax.all_gather(frames[None], "patch", axis=0, tiled=True)
    matched = (neighbour == own_index)[:, :, None] & (
        (seam_code % 4)[:, :, None] == sides[None, None, :]
    )
    keep_same = (matched & (seam_code < 4)[:, :, None]).astype(jnp.float32)
    keep_turned = (matched & (seam_code >= 4)[:, :, None]).astype(jnp.float32)
    running = jnp.einsum("rst,rsep->tep", keep_same, shard_rows, precision=lax.Precision.HIGHEST)
    edge_back = running + jnp.einsum(
        "rst,rsep->tep", keep_turned, shard_rows[..., ::-1], precision=lax.Precision.HIGHEST
    )
    grad_h = interior.at[:, 0, :].add(edge_back[0])
    grad_h = grad_h.at[:, -1, :].add(edge_back[1])
    grad_h = grad_h.at[:, :, 0].add(edge_back[2])
    grad_h = grad_h.at[:, :, -1].add(edge_back[3])
    grad_h = grad_h.reshape(inner_ch, cell_count)
    grad_pre = jax.vjp(smooth_gate, preact)[1](grad_h)[0]
    bias_local = jnp.sum(grad_pre, axis=1)
    pre_wide = widen(grad_pre.astype(jnp.bfloat16), length)
    one_local = jnp.stack(
        [
            lax.dot_general(
                pre_wide, x_taps[idx], (((1,), (1,)), ((), ())), preferred_element_type=jnp.float32
            )
            for idx in range(9)
        ]
    )
    two_local = jnp.stack(
        [
            lax.dot_general(
                grad_wide, h_taps[idx], (((1,), (1,)), ((), ())), preferred_element_type=jnp.float32
            )
            for idx in range(9)
        ]
    )
    grad_one, grad_two, grad_bias = lax.psum((one_local, two_local, bias_local), "patch")
    return (loss_value, grad_one, grad_two, grad_bias)


def solution(mesh):
    placed = (
        P("patch", "chan", None),
        P(None, "chan", None),
        P("chan"),
        P(None, None, "chan"),
        P(),
        P(),
        P(),
        P("patch", "chan", None),
        P("patch", None),
    )
    return jax.shard_map(
        on_device,
        mesh=mesh,
        in_specs=placed,
        out_specs=(P(), P(None, "chan", None), P(None, None, "chan"), P("chan")),
        check_vma=False,
    )
```

profile of v0, /device:TPU:0, one launch (start us, length us, event | category | flops | bytes accessed | tf_op | source)
XLA Modules:
  0.0 331.3 jit_solution(5937897365871116879)
XLA Ops:
  7.2 7.4 %all-gather = bf16[1,128,1024]{2,1,0:T(8,128)(2,1)S(1)} all-gather(bf16[1,64,1024]{2,1,0:T(8,128)(2,1)} %param.33), channel_id=2, replica_groups=mesh['patch'=16,'chan'=2] {'chan'}, dimensions={1}, use_global_device_ids=true | all-gather | bytes 393216 | tf_op jit(solution)/shard_map/all_gather | solution.py:91
  14.8 0.9 dynamic-slice_reduce_fusion
  15.8 23.5 %all-gather.1 = bf16[64,128,32]{1,2,0:T(8,128)(2,1)S(1)} all-gather(bf16[4,128,32]{1,2,0:T(8,128)(2,1)S(1)} %pad_maximum_fusion.2), channel_id=3, replica_groups=mesh['patch'=16,'chan'=2] {'patch'}, dimensions={0}, use_global_device_ids=true | all-gather | bytes 557056 | tf_op jit(solution)/shard_map/all_gather | solution.py:93
  39.3 0.5 convolution_bitcast_fusion.28
  40.0 0.6 fusion.174
  40.6 1.5 scatter.34
  45.7 0.5 copy-done.12
  46.7 0.6 pad_maximum_fusion.1
  47.8 35.0 %all-gather.7.cloned.1.call-done = bf16[64,256,32]{1,2,0:T(8,128)(2,1)} async-done(((bf16[4,256,32]{1,2,0:T(8,128)(2,1)}), bf16[64,256,32]{1,2,0:T(8,128)(2,1)}) %all-gather.7.cloned.1.call-update) | async-done | bytes 1048592 | tf_op jit(solution)/shard_map/all_gather | solution.py:101
  82.7 2.0 convolution_bitcast_fusion.27
  85.0 1.5 scatter.40
  90.3 1.0 copy.93
  91.5 13.4 %reduce-scatter.4.cloned.1.call-done = f32[64,1024]{1,0:T(8,128)} async-done(((f32[128,1024]{1,0:T(8,128)}), f32[64,1024]{1,0:T(8,128)}) %reduce-scatter.4.cloned.1.call-update) | async-done | bytes 262160
  104.9 1.1 copy.94
  106.3 1.0 reshape.635
  107.4 5.6 %all-to-all-start = ((f32[16,1,4096]{2,1,0:T(1,128)}), f32[16,1,4096]{2,1,0:T(1,128)S(1)}, u32[]{:S(2)}, u32[]{:S(2)}) async-start(f32[16,1,4096]{2,1,0:T(1,128)} %reshape.635), calls=%async_computation | async-start | bytes 524288 | tf_op jit(solution)/shard_map/all_to_all | solution.py:116
  113.3 0.6 scatter_custom_fusion
  114.0 9.1 %all-to-all-done = f32[16,1,4096]{2,1,0:T(1,128)S(1)} async-done(((f32[16,1,4096]{2,1,0:T(1,128)}), f32[16,1,4096]{2,1,0:T(1,128)S(1)}, u32[]{:S(2)}, u32[]{:S(2)}) %all-to-all-start) | async-done | bytes 262176 | tf_op jit(solution)/shard_map/all_to_all | solution.py:116
  123.0 0.5 broadcast.368
  123.6 1.3 reduce.35
  124.8 1.0 reshape.636
  125.9 1.6 gather_fusion
  127.7 0.6 gather_fusion.1
  128.6 10.7 %all_to_all.10 = bf16[16,2,2048]{2,1,0:T(2,128)(2,1)S(1)} all-to-all(bf16[16,2,2048]{2,1,0:T(2,128)(2,1)S(1)} %reshape.637), channel_id=1, replica_groups=mesh['patch'=16,'chan'=2] {'patch'}, dimensions={0} | all-to-all | bytes 262144 | tf_op jit(solution)/shard_map/all_to_all | solution.py:130
  139.9 5.6 %all_gather.18 = bf16[128,1024]{1,0:T(8,128)(2,1)S(1)} all-gather(bf16[64,1024]{1,0:T(8,128)(2,1)S(1)} %reshape.572), channel_id=1, replica_groups=mesh['patch'=16,'chan'=2] {'chan'}, dimensions={0}, use_global_device_ids=true | all-gather | bytes 393216 | tf_op jit(solution)/shard_map/all_gather | solution.py:135
  145.5 0.8 copy.79
  146.4 1.0 pad.104
  147.5 1.2 convolution_bitcast_fusion.6
  151.2 1.7 pad_add_fusion
  152.9 2.5 reshape.575
  155.4 0.8 fusion.170
  156.2 1.1 slice_bitcast_fusion.3
  157.5 0.7 copy.82
  158.3 2.4 slice.614
  160.7 0.9 fusion.20
  161.7 1.0 fusion.19
  162.7 1.0 fusion.18
  163.6 1.0 fusion.17
  164.6 1.0 fusion.16
  165.5 1.0 fusion.15
  166.5 1.0 fusion.14
  167.4 1.0 fusion.13
  168.4 1.0 fusion.12
  169.4 27.6 %all-gather.9.cloned.1.call-done = f32[64,256,32]{1,2,0:T(8,128)} async-done(((f32[4,256,32]{1,2,0:T(8,128)}), f32[64,256,32]{1,2,0:T(8,128)}) %all-gather.9.cloned.1.call-update) | async-done | bytes 2097168 | tf_op jit(solution)/shard_map/all_gather | solution.py:164
  197.0 3.9 %rev.11 = f32[16,4,256,32]{2,3,1,0:T(8,128)} reverse(f32[16,4,256,32]{2,3,1,0:T(8,128)} %bitcast.319), dimensions={3} | reverse | bytes 4194304 | tf_op jit(solution)/shard_map/rev | solution.py:172
  200.8 3.6 %fusion.6 = f32[4,256,32]{1,0,2:T(4,128)S(1)} fusion(f32[16,4,256,32]{2,3,1,0:T(8,128)} %bitcast.320, s32[16,4]{0,1:T(4,128)S(1)} %add_select_fusion, pred[16,4]{0,1:T(4,128)(4,1)S(1)} %get-tuple-element.175, pred[16,4]{0,1:T(4,128)(4,1)S(1)} %get-tuple-element.182), kind=kOutput, calls=%fused_computation.43 | convolution fusion | flops 25166592 | bytes 2228608 | tf_op jit(solution)/shard_map/rst,rsep->tep/dot_general | solution.py:170
  204.5 2.0 fusion.30
  206.6 1.4 fusion.134
  208.0 1.4 fusion.133
  209.3 1.0 fusion.132
  210.3 1.8 scatter-add.16
  212.1 1.0 fusion.131
  213.1 1.8 scatter-add.19
  214.9 2.0 fusion.168
  217.1 0.4 fusion.29
  219.0 0.4 fusion.24
  220.6 1.0 copy-done.4
  222.1 0.4 copy-done.8
  222.5 0.7 fusion.59
  223.2 38.6 %psum.28 = f32[]{:T(128)} all-reduce(f32[]{:T(128)} %fusion.59), channel_id=1, replica_groups=mesh['patch'=16,'chan'=2] {'patch','chan'}, use_global_device_ids=true, to_apply=%region_2.3 | all-reduce | flops 1 | bytes 8 | tf_op jit(solution)/shard_map/psum | solution.py:134
  262.4 32.4 %psum.31 = f32[256]{0:T(256)} all-reduce(f32[256]{0:T(256)S(1)} %get-tuple-element.150), channel_id=1, replica_groups=mesh['patch'=16,'chan'=2] {'patch'}, use_global_device_ids=true, to_apply=%region_7.8 | all-reduce | flops 256 | bytes 2048 | tf_op jit(solution)/shard_map/psum | solution.py:198
  294.8 25.3 %all-reduce.18.cloned.1.call-done = (f32[9,256,128]{2,1,0:T(8,128)}, f32[9,128,256]{2,1,0:T(8,128)}) async-done(((f32[9,256,128]{2,1,0:T(8,128)}, f32[9,128,256]{2,1,0:T(8,128)}), (f32[9,256,128]{2,1,0:T(8,128)}, f32[9,128,256]{2,1,0:T(8,128)})) %all-reduce.18.cloned.1.call-update) | async-done | bytes 2359312 | tf_op jit(solution)/shard_map/psum | solution.py:198
  320.2 2.5 copy.182
  322.6 1.0 copy.183
  (132 shorter events, 17.0 us)
Async XLA Ops:
  7.2 75.6 %all-gather.7.cloned.1.call-start = ((), (), s32[]{:S(2)}) async-start(), calls=%async_computation.3 | async-start | bytes 1114112 | tf_op jit(solution)/shard_map/all_gather | solution.py:101
  39.2 3.4 %copy-start.5 = (bf16[9,256,128]{2,1,0:T(8,128)(2,1)S(1)}, bf16[9,256,128]{2,1,0:T(8,128)(2,1)}, u32[]{:S(2)}) copy-start(bf16[9,256,128]{2,1,0:T(8,128)(2,1)} %param.34) | copy-start | bytes 1769476
  45.5 0.7 copy-start.12
  47.4 57.6 %reduce-scatter.4.cloned.1.call-start = ((), (), s32[]{:S(2)}) async-start(), calls=%async_computation.5 | async-start | bytes 786432
  84.7 2.5 copy-start.1
  90.2 1.0 copy-start.6
  90.3 1.2 copy-start.13
  106.1 6.9 %copy-start.10 = (bf16[1,1024]{1,0:T(2,128)(2,1)S(1)}, bf16[1,1024]{1,0:T(2,128)(2,1)}, u32[]{:S(2)}) copy-start(bf16[1,1024]{1,0:T(2,128)(2,1)} %param.41) | copy-start | bytes 6148
  106.1 7.0 %copy-start.7 = (bf16[1,64,1024]{2,1,0:T(8,128)(2,1)S(1)}, bf16[1,64,1024]{2,1,0:T(8,128)(2,1)}, u32[]{:S(2)}) copy-start(bf16[1,64,1024]{2,1,0:T(8,128)(2,1)} %param.40) | copy-start | bytes 393220
  107.4 15.7 %all-to-all-start = ((f32[16,1,4096]{2,1,0:T(1,128)}), f32[16,1,4096]{2,1,0:T(1,128)S(1)}, u32[]{:S(2)}, u32[]{:S(2)}) async-start(f32[16,1,4096]{2,1,0:T(1,128)} %reshape.635), calls=%async_computation | async-start | bytes 524288 | tf_op jit(solution)/shard_map/all_to_all | solution.py:116
  113.0 84.0 %all-gather.9.cloned.1.call-start = ((), (), s32[]{:S(2)}) async-start(), calls=%async_computation.4 | async-start | bytes 2228224 | tf_op jit(solution)/shard_map/all_gather | solution.py:164
  147.4 1.2 copy-start.2
  152.9 5.3 %copy-start.9 = (s32[16,4]{0,1:T(4,128)S(1)}, s32[16,4]{0,1:T(4,128)}, u32[]{:S(2)}) copy-start(s32[16,4]{0,1:T(4,128)} %param.38) | copy-start | bytes 772
  152.9 5.4 %copy-start.11 = (s32[16,4]{0,1:T(4,128)S(1)}, s32[16,4]{0,1:T(4,128)}, u32[]{:S(2)}) copy-start(s32[16,4]{0,1:T(4,128)} %param.37) | copy-start | bytes 772
  158.2 162.0 %all-reduce.18.cloned.1.call-start = ((), (), s32[]{:S(2)}) async-start(), calls=%async_computation.6 | async-start | bytes 4718592 | tf_op jit(solution)/shard_map/psum | solution.py:198
  200.8 3.6 %copy-start = (f32[16,4,256,32]{2,3,1,0:T(8,128)S(1)}, f32[16,4,256,32]{2,3,1,0:T(8,128)}, u32[]{:S(2)}) copy-start(f32[16,4,256,32]{2,3,1,0:T(8,128)} %rev.11) | copy-start | bytes 6291460
  220.6 1.0 copy-start.4
  221.6 0.9 copy-start.8
  320.2 2.5 copy-start.3
Sparse Core Ops, SparseCore 0:
  47.5 35.2 all-gather.6
  91.4 13.4 reduce-scatter.3
  158.3 38.5 all-gather.8
  221.7 98.3 all-reduce.17
where the time goes:
time: 332 us; the launch traced here: 331 us
  blocking collectives  118 us (36%)
  waiting for transfers between devices  110 us (33%)
  local copies, waits for them, and re-layouts  38.7 us (12%)
  matrix products  29.4 us (9%)
  between operations  16.4 us (5%)
  other arithmetic  12.4 us (4%)
  starting transfers between devices  5.79 us (2%)
    psum x1, blocking collectives, on_device(): lax.psum(partial_loss, ('patch', 'chan')) / (patch_count * cell_count * C)  38.6 us
    all_gather x1, waiting for transfers between devices, on_device(): lax.all_gather(edges_of(hidden_grid)[None], 'patch', axis=0, tiled=True)  35 us
    psum x1, blocking collectives, on_device(): lax.psum((one_local, two_local, bias_local), 'patch')  32.4 us
    all_gather x1, waiting for transfers between devices, on_device(): shard_rows = lax.all_gather(frames[None], 'patch', axis=0, tiled=True)  27.6 us
    psum x1, waiting for transfers between devices, on_device(): lax.psum((one_local, two_local, bias_local), 'patch')  25.3 us
    all_gather x1, blocking collectives, on_device(): lax.all_gather(edges_of(grid)[None], 'patch', axis=0, tiled=True)  23.5 us
    unnamed x5, waiting for transfers between devices  13.5 us
    all_to_all x1, blocking collectives, on_device(): lax.all_to_all(band_grad[:, inverse, :], 'patch', split_axis=1, concat_ax...  10.7 us
  transfers between devices with their start and end apart: 5, of which 5 were waited for; matrix products, arithmetic and copies ran while one was open for 4% of the time, Pallas kernels for 0%

commit v1 on v0

v1 whole, which is shorter than its diff:
```python
import math

import jax
import jax.numpy as jnp
from jax import lax
from jax.sharding import PartitionSpec as P

P_SIZE = 32


def edges_of(grid):
    return jnp.stack([grid[0], grid[-1], grid[:, 0], grid[:, -1]])


def with_frame(grid, strips):
    rows = jnp.concatenate([strips[0][None], grid, strips[1][None]], axis=0)
    left = jnp.pad(strips[2], ((1, 1), (0, 0)))[:, None]
    right = jnp.pad(strips[3], ((1, 1), (0, 0)))[:, None]
    return jnp.concatenate([left, rows, right], axis=1)


def conv(values, weight, pad, spec):
    return lax.conv_general_dilated(
        values[None],
        weight,
        (1, 1),
        ((pad, pad), (pad, pad)),
        dimension_numbers=("NHWC", spec, "NHWC"),
        preferred_element_type=jnp.float32,
    )[0]


def smooth_gate(values):
    return jax.nn.gelu(values, approximate=True)


def on_device(fields, w_one, bias_one, w_two, neighbour, seam_code, band_order, target, lat_weight):
    length = P_SIZE
    cells = length * length
    count = lax.axis_size("patch")
    chans = lax.axis_size("chan")
    part = cells // count
    own = lax.axis_index("patch")
    own_nbr = lax.dynamic_slice_in_dim(neighbour, own, 1, 0)[0]
    own_code = lax.dynamic_slice_in_dim(seam_code, own, 1, 0)[0]
    ids = jnp.arange(count, dtype=jnp.int32)
    faces = (own_nbr[:, None] == ids[None, :]).astype(jnp.bfloat16)
    turned = (own_code >= 4)[:, None, None]
    inner = w_one.shape[1]

    def to_send(grid):
        strips = edges_of(grid)
        strips = jnp.where(turned, strips[:, ::-1], strips)
        return jnp.einsum(
            "tr,tkc->rkc", faces, strips, preferred_element_type=jnp.float32
        ).astype(jnp.bfloat16)

    def picked(arrived):
        return jnp.einsum(
            "tr,rkc->tkc", faces, arrived, preferred_element_type=jnp.float32
        ).astype(jnp.bfloat16)

    def swap(sent):
        return lax.all_to_all(sent, "patch", split_axis=0, concat_axis=0, tiled=True)

    both = lax.all_gather(jnp.stack([fields[0], target[0]]), "chan", axis=1, tiled=True)
    chan_full = both.shape[1]
    x_grid = both[0].T.reshape(length, length, chan_full)
    slots = (band_order[None, :] == ids[:, None]).astype(jnp.bfloat16)
    lat_rows = -(-part // chan_full)
    lat_parts = jnp.pad(
        lat_weight.reshape(count, part), ((0, 0), (0, lat_rows * chan_full - part))
    ).reshape(count, lat_rows, chan_full)
    band_parts = jnp.concatenate(
        [both[1].T.reshape(count, part, chan_full), lat_parts], axis=1
    )
    band_parts = jnp.einsum(
        "ps,skc->pkc", slots, band_parts, preferred_element_type=jnp.float32
    ).astype(jnp.bfloat16)
    first = swap(jnp.concatenate([to_send(x_grid), band_parts], axis=1))
    x_pad = with_frame(x_grid, picked(first[:, :length]))
    target_patch = first[:, length : length + part].reshape(cells, chan_full)
    lat_w = (
        first[:, length + part :].reshape(count, lat_rows * chan_full)[:, :part].reshape(cells, 1)
    ).astype(jnp.float32)

    preact = conv(x_pad, w_one.reshape(3, 3, inner, chan_full), 0, "HWOI") + bias_one
    hidden = smooth_gate(preact).astype(jnp.bfloat16)
    h_pad = with_frame(hidden, picked(swap(to_send(hidden))))
    partial = conv(h_pad, w_two.reshape(3, 3, chan_full, inner), 0, "HWOI").reshape(
        cells, chan_full
    )
    mixed = partial
    rounded = partial.astype(jnp.bfloat16)
    for shift in range(1, chans):
        mixed = mixed + lax.ppermute(
            rounded, "chan", [(i, (i + shift) % chans) for i in range(chans)]
        ).astype(jnp.float32)
    x_flat = x_grid.reshape(cells, chan_full)
    misfit = x_flat.astype(jnp.float32) + mixed - target_patch.astype(jnp.float32)
    weighted = lat_w * misfit
    loss_local = jnp.sum(weighted * misfit)
    inv_root = 1.0 / math.sqrt(count * cells)
    grad_out = (weighted * inv_root).astype(jnp.bfloat16)
    g_grid = grad_out.reshape(length, length, chan_full)

    h_taps = [
        h_pad[a : a + length, b : b + length].reshape(cells, inner)
        for a in range(3)
        for b in range(3)
    ]
    two_local = jnp.stack(
        [
            lax.dot_general(
                grad_out, tap, (((0,), (0,)), ((), ())), preferred_element_type=jnp.float32
            )
            for tap in h_taps
        ]
    )

    near = picked(swap(to_send(g_grid)))
    side_taps = jnp.array([[0, 1, 2], [6, 7, 8], [0, 3, 6], [2, 5, 8]], jnp.int32)
    used = side_taps[own_code % 4]
    used = jnp.where((own_code >= 4)[:, None], used[:, ::-1], used)
    hot = (used[:, :, None] == jnp.arange(9)[None, None, :]).astype(jnp.bfloat16)
    spread = jnp.pad(near, ((0, 0), (1, 1), (0, 0)))
    shifted = jnp.stack([spread[:, 2 - d : 2 - d + length] for d in range(3)], axis=1)
    side_in = jnp.einsum(
        "tdn,tdkc->tknc", hot, shifted, preferred_element_type=jnp.float32
    ).astype(jnp.bfloat16)
    back = lax.dot_general(
        side_in.reshape(4 * length, 9 * chan_full),
        w_two.reshape(9 * chan_full, inner),
        (((1,), (0,)), ((), ())),
        preferred_element_type=jnp.float32,
    ).reshape(4, length, inner)
    grad_h = conv(g_grid, w_two.reshape(3, 3, chan_full, inner)[::-1, ::-1], 1, "HWIO")
    row = lax.broadcasted_iota(jnp.int32, (length, length, 1), 0)
    col = lax.broadcasted_iota(jnp.int32, (length, length, 1), 1)
    grad_h = (
        grad_h
        + jnp.where(row == 0, back[0][None], 0.0)
        + jnp.where(row == length - 1, back[1][None], 0.0)
        + jnp.where(col == 0, back[2][:, None], 0.0)
        + jnp.where(col == length - 1, back[3][:, None], 0.0)
    )
    grad_pre = jax.vjp(smooth_gate, preact)[1](grad_h)[0].reshape(cells, inner)
    bias_local = jnp.sum(grad_pre, axis=0)
    pre_b = grad_pre.astype(jnp.bfloat16)
    x_taps = [
        x_pad[a : a + length, b : b + length].reshape(cells, chan_full)
        for a in range(3)
        for b in range(3)
    ]
    one_local = jnp.stack(
        [
            lax.dot_general(
                pre_b, tap, (((0,), (0,)), ((), ())), preferred_element_type=jnp.float32
            )
            for tap in x_taps
        ]
    )
    small_rows = -(-inner // chan_full) + 1
    small = jnp.concatenate(
        [
            jnp.pad(bias_local, (0, (small_rows - 1) * chan_full - inner)),
            jnp.pad(loss_local[None], (0, chan_full - 1)),
        ]
    ).reshape(small_rows, chan_full)
    sum_two = lax.psum(two_local, "patch")
    sums = lax.psum(
        jnp.concatenate([one_local.reshape(9 * inner, chan_full), small], axis=0), "patch"
    )
    grad_one = sums[: 9 * inner].reshape(9, inner, chan_full)
    grad_bias = sums[9 * inner : -1].reshape(-1)[:inner]
    loss_value = sums[-1, 0] / (count * cells * chan_full)
    return (loss_value, grad_one, sum_two, grad_bias)


def solution(mesh):
    placed = (
        P("patch", "chan", None),
        P(None, "chan", None),
        P("chan"),
        P(None, None, "chan"),
        P(),
        P(),
        P(),
        P("patch", "chan", None),
        P("patch", None),
    )
    return jax.shard_map(
        on_device,
        mesh=mesh,
        in_specs=placed,
        out_specs=(P(), P(None, "chan", None), P(None, None, "chan"), P("chan")),
        check_vma=False,
    )
```

time: 332 us -> 234 us (0.70)
  blocking collectives: 118 us -> 9.91 us
  starting transfers between devices: 5.79 us -> 18 us
  matrix products: 29.4 us -> 23.1 us
  waiting for transfers between devices: 110 us -> 114 us
    psum x1, waiting for transfers between devices: 25.3 us -> 101 us  [on_device(): lax.psum(jnp.concatenate([one_local.reshape(9 * inner, chan_full), small]...]
    psum x2 -> x0, blocking collectives: 71 us -> none  [the longest x1 38.6 us: on_device(): lax.psum(partial_loss, ('patch', 'chan')) / (patch_count * cell_count * C)]
    all_gather x2 -> x0, waiting for transfers between devices: 62.6 us -> none  [the longest x1 35 us: on_device(): lax.all_gather(edges_of(hidden_grid)[None], 'patch', axis=0, tiled=True)]
    all_gather x3 -> x1, blocking collectives: 36.5 us -> 9.91 us  [on_device(): lax.all_gather(jnp.stack([fields[0], target[0]]), 'chan', axis=1, tiled=T...]
    unnamed x5 -> x1, waiting for transfers between devices: 13.5 us -> 0.02 us
    dot_general x49 -> x27, matrix products: 29.4 us -> 18 us  [the longest x9 9.39 us: on_device(): lax.dot_general(grad_out, tap, (((0,), (0,)), ((), ())), preferred_elemen...]
    all_to_all x1 -> x3, starting transfers between devices: 5.62 us -> 16.4 us  [swap(): lax.all_to_all(sent, 'patch', split_axis=0, concat_axis=0, tiled=True)]
    all_to_all x1 -> x0, blocking collectives: 10.7 us -> none  [on_device(): lax.all_to_all(band_grad[:, inverse, :], 'patch', split_axis=1, concat_ax...]
  transfers between devices with their start and end apart: 5 -> 5, of which waited for: 5 -> 3; matrix products, arithmetic and copies ran while one was open for 4% -> 11% of each run, Pallas kernels for 0% -> 0%
where the time goes in v1:
time: 234 us; the launch traced here: 233 us
  waiting for transfers between devices  114 us (49%)
  local copies, waits for them, and re-layouts  36.7 us (16%)
  matrix products  23.1 us (10%)
  starting transfers between devices  18 us (8%)
  between operations  16.8 us (7%)
  other arithmetic  15.3 us (7%)
  blocking collectives  9.91 us (4%)
    psum x1, waiting for transfers between devices, on_device(): lax.psum(jnp.concatenate([one_local.reshape(9 * inner, chan_full), small]...  101 us
    all_to_all x3, starting transfers between devices, swap(): lax.all_to_all(sent, 'patch', split_axis=0, concat_axis=0, tiled=True)  16.4 us
    all_to_all x3, waiting for transfers between devices, swap(): lax.all_to_all(sent, 'patch', split_axis=0, concat_axis=0, tiled=True)  10.8 us
    all_gather x1, blocking collectives, on_device(): lax.all_gather(jnp.stack([fields[0], target[0]]), 'chan', axis=1, tiled=T...  9.91 us
    dot_general x9, matrix products, on_device(): lax.dot_general(grad_out, tap, (((0,), (0,)), ((), ())), preferred_elemen...  9.39 us
    unnamed x85, local copies, waits for them, and re-layouts  6.32 us
    conv_general_dilated x13, local copies, waits for them, and re-layouts, conv(): lax.conv_general_dilated(values[None], weight, (1, 1), ((pad, pad), (pad,...  6.06 us
    slice x10, local copies, waits for them, and re-layouts, on_device(): h_pad[a:a + length, b:b + length].reshape(cells, inner)  5.55 us
  transfers between devices with their start and end apart: 5, of which 3 were waited for; matrix products, arithmetic and copies ran while one was open for 11% of the time, Pallas kernels for 0%

profile of v1, /device:TPU:0, one launch (start us, length us, event | category | flops | bytes accessed | tf_op | source)
XLA Modules:
  0.0 233.3 jit_solution(5168928998311883322)
XLA Ops:
  7.2 1.2 copy.213
  8.4 1.1 copy.214
  9.5 0.6 pad_maximum_fusion.8
  10.1 9.9 %all_gather.3 = bf16[2,128,1024]{2,0,1:T(2,128)(2,1)S(1)} all-gather(bf16[2,64,1024]{2,0,1:T(2,128)(2,1)S(1)} %pad_maximum_fusion.8), channel_id=1, replica_groups=mesh['patch'=16,'chan'=2] {'chan'}, dimensions={1}, use_global_device_ids=true | all-gather | bytes 786432 | tf_op jit(solution)/shard_map/all_gather | solution.py:66
  20.0 0.7 fusion.121
  20.7 0.4 copy.274
  21.7 0.4 copy.275
  23.2 0.9 copy.219
  24.0 6.2 %all-to-all-start = ((bf16[16,97,128]{2,1,0:T(8,128)(2,1)}), bf16[16,97,128]{2,1,0:T(8,128)(2,1)S(1)}, u32[]{:S(2)}, u32[]{:S(2)}) async-start(bf16[16,97,128]{2,1,0:T(8,128)(2,1)} %copy.219), calls=%async_computation | async-start | bytes 851968 | tf_op jit(solution)/shard_map/all_to_all | solution.py:64
  30.3 0.6 gather_fusion
  30.9 0.6 iota_compare_fusion.7
  31.5 0.7 broadcast_select_fusion.3
  32.2 10.8 %all-to-all-done = bf16[16,97,128]{2,1,0:T(8,128)(2,1)S(1)} async-done(((bf16[16,97,128]{2,1,0:T(8,128)(2,1)}), bf16[16,97,128]{2,1,0:T(8,128)(2,1)S(1)}, u32[]{:S(2)}, u32[]{:S(2)}) %all-to-all-start) | async-done | bytes 397344 | tf_op jit(solution)/shard_map/all_to_all | solution.py:64
  44.3 2.3 subtract_multiply_fusion
  47.5 1.0 slice.267
  48.5 1.4 add_multiply_fusion
  50.0 1.5 copy.250
  51.7 0.9 pad_maximum_fusion.6
  52.7 0.8 broadcast_select_fusion
  53.9 0.8 copy.233
  54.7 4.4 %all-to-all-start.1 = ((bf16[16,32,256]{2,1,0:T(8,128)(2,1)}), bf16[16,32,256]{2,1,0:T(8,128)(2,1)}, u32[]{:S(2)}, u32[]{:S(2)}) async-start(bf16[16,32,256]{2,1,0:T(8,128)(2,1)} %copy.233), calls=%async_computation.1 | async-start | bytes 524288 | tf_op jit(solution)/shard_map/all_to_all | solution.py:64
  59.1 0.8 slice.259
  59.9 1.9 copy.262
  61.9 1.5 copy.249
  63.4 1.5 copy.252
  64.8 1.5 copy.251
  66.3 1.0 fusion.123
  67.3 1.0 fusion.122
  68.3 1.1 fusion.38
  69.4 1.2 convolution_convert_fusion.5
  70.8 0.5 pad_maximum_fusion.1
  71.7 0.4 pad_maximum_fusion.2
  73.2 0.8 copy-done.19
  74.0 1.7 convolution_select_fusion.2
  76.2 1.6 collective-permute-start
  78.5 1.1 copy.260
  79.5 1.1 copy.261
  81.6 1.1 copy.266
  82.7 1.9 collective-permute-done
  84.6 0.8 fusion.58
  85.4 0.9 fusion.13
  86.7 1.0 convolution_select_fusion
  87.7 1.7 copy.242
  89.9 0.7 copy.246
  90.6 5.9 %all-to-all-start.2 = ((bf16[16,32,128]{2,1,0:T(8,128)(2,1)}), bf16[16,32,128]{2,1,0:T(8,128)(2,1)}, u32[]{:S(2)}, u32[]{:S(2)}) async-start(bf16[16,32,128]{2,1,0:T(8,128)(2,1)} %copy.246), calls=%async_computation.2 | async-start | bytes 262144 | tf_op jit(solution)/shard_map/all_to_all | solution.py:64
  96.5 0.9 fusion.12
  97.5 2.0 fusion.11
  99.4 0.9 fusion.10
  100.4 0.9 fusion.9
  101.3 0.9 fusion.8
  102.2 0.9 fusion.7
  103.1 0.9 fusion.6
  104.1 0.9 fusion.5
  105.0 1.2 convolution_convert_fusion.6
  106.4 0.4 convolution_convert_fusion
  106.8 1.3 fusion.74
  108.2 3.8 %fusion.116 = (bf16[1,32,32,256]{3,1,2,0:T(8,128)(2,1)S(1)}, f32[1,32,32,256]{3,1,2,0:T(8,128)}) fusion(f32[32,1,40,256]{3,0,2,1:T(8,128)} %bitcast.352, f32[32,1,40,256]{3,0,2,1:T(8,128)} %bitcast.353, f32[32,1,40,256]{3,0,2,1:T(8,128)S(1)} %bitcast.350, f32[32,1,40,256]{3,0,2,1:T(8,128)S(1)} %bitcast.351, f32[32,256]{1,0:T(8,128)S(1)} %get-tuple-element.49, ...), kind=kLoop, calls=%fused_computation.217 | loop fusion | flops 4718592 | bytes 6948864 | tf_op jit(solution)/shard_map/convert_element_type | solution.py:149
  116.1 0.7 fusion.99
  116.8 1.1 pad_maximum_fusion
  117.9 100.8 %all-reduce.10.cloned.1.call-done = (f32[2307,128]{1,0:T(8,128)}, f32[9,128,256]{2,1,0:T(8,128)}) async-done(((f32[2307,128]{1,0:T(8,128)}, f32[9,128,256]{2,1,0:T(8,128)}), (f32[2307,128]{1,0:T(8,128)}, f32[9,128,256]{2,1,0:T(8,128)})) %all-reduce.10.cloned.1.call-update) | async-done | bytes 2360848 | tf_op jit(solution)/shard_map/psum | solution.py:171
  218.8 2.5 %slice.300 = f32[2304,128]{1,0:T(8,128)} slice(f32[2307,128]{1,0:T(8,128)} %get-tuple-element.4), slice={[0:2304], [0:128]} | slice | bytes 2359296 | tf_op jit(solution)/shard_map/slice | solution.py:174
  221.2 1.2 slice.299
  222.4 1.2 slice_bitcast_fusion.13
  224.3 1.0 copy.337
  (166 shorter events, 12.9 us)
Async XLA Ops:
  7.2 36.7 %copy-start = (bf16[9,256,128]{2,1,0:T(8,128)(2,1)S(1)}, bf16[9,256,128]{2,1,0:T(8,128)(2,1)}, u32[]{:S(2)}) copy-start(bf16[9,256,128]{2,1,0:T(8,128)(2,1)} %param.11) | copy-start | bytes 1769476
  20.0 1.3 copy-start.24
  20.0 1.5 copy-start.30
  20.7 1.7 copy-start.25
  20.7 2.2 copy-start.31
  23.1 7.2 %copy-start.22 = (s32[4,3]{1,0:T(4,128)S(1)}, s32[4,3]{1,0:T(4,128)}, u32[]{:S(2)}) copy-start(s32[4,3]{1,0:T(4,128)} %constant.54.clone) | copy-start | bytes 148
  24.0 18.9 %all-to-all-start = ((bf16[16,97,128]{2,1,0:T(8,128)(2,1)}), bf16[16,97,128]{2,1,0:T(8,128)(2,1)S(1)}, u32[]{:S(2)}, u32[]{:S(2)}) async-start(bf16[16,97,128]{2,1,0:T(8,128)(2,1)} %copy.219), calls=%async_computation | async-start | bytes 851968 | tf_op jit(solution)/shard_map/all_to_all | solution.py:64
  43.0 0.8 copy-start.8
  43.6 0.7 copy-start.26
  43.6 0.7 copy-start.32
  47.5 5.1 %copy-start.20 = (bf16[1,32,256]{2,1,0:T(8,128)(2,1)}, bf16[1,32,256]{2,1,0:T(8,128)(2,1)S(1)}, u32[]{:S(2)}) copy-start(bf16[1,32,256]{2,1,0:T(8,128)(2,1)S(1)} %get-tuple-element.26) | copy-start | bytes 49156
  47.5 5.1 %copy-start.21 = (bf16[1,32,256]{2,1,0:T(8,128)(2,1)}, bf16[1,32,256]{2,1,0:T(8,128)(2,1)S(1)}, u32[]{:S(2)}) copy-start(bf16[1,32,256]{2,1,0:T(8,128)(2,1)S(1)} %get-tuple-element.27) | copy-start | bytes 49156
  54.7 14.8 %all-to-all-start.1 = ((bf16[16,32,256]{2,1,0:T(8,128)(2,1)}), bf16[16,32,256]{2,1,0:T(8,128)(2,1)}, u32[]{:S(2)}, u32[]{:S(2)}) async-start(bf16[16,32,256]{2,1,0:T(8,128)(2,1)} %copy.233), calls=%async_computation.1 | async-start | bytes 524288 | tf_op jit(solution)/shard_map/all_to_all | solution.py:64
  59.9 1.9 copy-start.1
  63.4 1.5 copy-start.9
  67.3 1.0 copy-start.27
  72.9 1.1 copy-start.19
  72.9 1.1 copy-start.33
  76.2 8.3 %collective-permute-start = (bf16[1024,128]{1,0:T(8,128)(2,1)S(1)}, bf16[1024,128]{1,0:T(8,128)(2,1)S(1)}, u32[]{:S(2)}, u32[]{:S(2)}) collective-permute-start(bf16[1024,128]{1,0:T(8,128)(2,1)S(1)} %bitcast_convert_fusion), channel_id=1, source_target_pairs={{0,1},{1,0},{2,3},{3,2},{4,5},{5,4},{6,7},{7,6},{8,9},{9,8},{10,11... | collective-permute-start | bytes 786440 | tf_op jit(solution)/shard_map/ppermute | solution.py:96
  81.3 3.3 %slice-start = ((bf16[16,97,128]{2,1,0:T(8,128)(2,1)}), bf16[16,64,128]{2,1,0:T(8,128)(2,1)S(1)}, s32[]{:S(2)}) async-start(bf16[16,97,128]{2,1,0:T(8,128)(2,1)} %copy-done.8), calls=%async_computation.4 | async-start | bytes 524288 | tf_op jit(solution)/shard_map/slice | solution.py:82
  90.6 14.4 %all-to-all-start.2 = ((bf16[16,32,128]{2,1,0:T(8,128)(2,1)}), bf16[16,32,128]{2,1,0:T(8,128)(2,1)}, u32[]{:S(2)}, u32[]{:S(2)}) async-start(bf16[16,32,128]{2,1,0:T(8,128)(2,1)} %copy.246), calls=%async_computation.2 | async-start | bytes 262144 | tf_op jit(solution)/shard_map/all_to_all | solution.py:64
  96.4 122.3 %all-reduce.10.cloned.1.call-start = ((), (), s32[]{:S(2)}) async-start(), calls=%async_computation.3 | async-start | bytes 4726784 | tf_op jit(solution)/shard_map/psum | solution.py:171
  96.5 2.9 %copy-start.6 = (bf16[32,32,256]{2,1,0:T(8,128)(2,1)S(1)}, bf16[32,32,256]{2,1,0:T(8,128)(2,1)}, u32[]{:S(2)}) copy-start(bf16[32,32,256]{2,1,0:T(8,128)(2,1)} %copy.261) | copy-start | bytes 1572868
  96.5 3.8 %copy-start.7 = (bf16[1024,256]{1,0:T(8,128)(2,1)S(1)}, bf16[1024,256]{1,0:T(8,128)(2,1)}, u32[]{:S(2)}) copy-start(bf16[1024,256]{1,0:T(8,128)(2,1)} %fusion.38) | copy-start | bytes 1572868
  101.3 2.8 %copy-start.5 = (bf16[32,32,256]{2,1,0:T(8,128)(2,1)S(1)}, bf16[32,32,256]{2,1,0:T(8,128)(2,1)}, u32[]{:S(2)}) copy-start(bf16[32,32,256]{2,1,0:T(8,128)(2,1)} %copy.266) | copy-start | bytes 1572868
  103.1 3.2 %copy-start.23 = (s32[4,3]{1,0:T(4,128)S(1)}, s32[4,3]{1,0:T(4,128)}, u32[]{:S(2)}) copy-start(s32[4,3]{1,0:T(4,128)} %broadcast_select_fusion.3) | copy-start | bytes 148
  104.1 4.1 %copy-start.3 = (f32[32,8,5,256]{3,0,2,1:T(8,128)S(1)}, f32[32,8,5,256]{3,0,2,1:T(8,128)}, u32[]{:S(2)}) copy-start(f32[32,8,5,256]{3,0,2,1:T(8,128)} %copy.249) | copy-start | bytes 3932164
  105.0 3.1 %copy-start.2 = (f32[32,8,5,256]{3,0,2,1:T(8,128)S(1)}, f32[32,8,5,256]{3,0,2,1:T(8,128)}, u32[]{:S(2)}) copy-start(f32[32,8,5,256]{3,0,2,1:T(8,128)} %copy.250) | copy-start | bytes 3932164
  105.0 3.1 %copy-start.28 = (pred[32]{0:T(512)(128)(4,1)S(1)}, pred[32]{0:T(512)(128)(4,1)}, u32[]{:S(2)}) copy-start(pred[32]{0:T(512)(128)(4,1)} %get-tuple-element.67) | copy-start | bytes 100
  105.0 3.2 %copy-start.29 = (pred[32]{0:T(512)(128)(4,1)S(1)}, pred[32]{0:T(512)(128)(4,1)}, u32[]{:S(2)}) copy-start(pred[32]{0:T(512)(128)(4,1)} %get-tuple-element.68) | copy-start | bytes 100
  108.2 4.1 %copy-start.17 = (bf16[32,32,128]{2,1,0:T(8,128)(2,1)S(1)}, bf16[32,32,128]{2,1,0:T(8,128)(2,1)}, u32[]{:S(2)}) copy-start(bf16[32,32,128]{2,1,0:T(8,128)(2,1)} %get-tuple-element.35) | copy-start | bytes 786436
  111.9 0.9 copy-start.12
  112.0 1.3 copy-start.18
  112.3 1.3 copy-start.15
  113.3 1.1 copy-start.16
  113.6 1.1 copy-start.13
  114.0 1.1 copy-start.11
  114.3 1.1 copy-start.14
  114.7 1.3 copy-start.4
  218.8 5.5 %copy-start.10 = (f32[9,128,256]{2,1,0:T(8,128)S(1)}, f32[9,128,256]{2,1,0:T(8,128)}, u32[]{:S(2)}) copy-start(f32[9,128,256]{2,1,0:T(8,128)} %get-tuple-element.71) | copy-start | bytes 3538948
Sparse Core Ops, SparseCore 0:
  118.0 100.6 all-reduce.9

commit v2 on v1

--- a/solution.py
+++ b/solution.py
@@ -3,6 +3,8 @@
 import jax
 import jax.numpy as jnp
 from jax import lax
+from jax.experimental import pallas as pl
+from jax.experimental.pallas import tpu as pltpu
 from jax.sharding import PartitionSpec as P
 
 P_SIZE = 32
@@ -32,6 +34,155 @@
 
 def smooth_gate(values):
     return jax.nn.gelu(values, approximate=True)
+
+
+def bits_of(size):
+    return [1 << k for k in range(size.bit_length() - 1)]
+
+
+def peer_of(place, bit):
+    return place + bit - 2 * bit * (lax.div(place, bit) % 2)
+
+
+def sum_kernel(count, chans, a_in, b_in, s_in, a_out, b_out, s_out, a_rec, b_rec, s_rec, send, recv):
+    place = lax.axis_index("patch")
+    lane = lax.axis_index("chan")
+    bits = bits_of(count)
+    swapped = bits if len(bits) < 3 else [bits[0], bits[2], bits[1]] + bits[3:]
+    chan_bits = bits_of(chans)
+    stages = len(bits)
+
+    def target(bit):
+        return {"patch": peer_of(place, bit)}
+
+    barrier = pltpu.get_barrier_semaphore()
+    for bit in bits:
+        pl.semaphore_signal(
+            barrier, inc=1, device_id=target(bit), device_id_type=pl.DeviceIdType.MESH
+        )
+    for bit in chan_bits:
+        pl.semaphore_signal(
+            barrier,
+            inc=1,
+            device_id={"chan": peer_of(lane, bit)},
+            device_id_type=pl.DeviceIdType.MESH,
+        )
+    pl.semaphore_wait(barrier, stages + len(chan_bits))
+
+    slot = [0]
+
+    def send_to(src, dst, device):
+        k = slot[0]
+        slot[0] = k + 1
+        copy = pltpu.make_async_remote_copy(
+            src_ref=src,
+            dst_ref=dst,
+            send_sem=send.at[k],
+            recv_sem=recv.at[k],
+            device_id=device,
+            device_id_type=pl.DeviceIdType.MESH,
+        )
+        copy.start()
+        return copy
+
+    s_out[...] = s_in[...]
+    streams = [
+        {"in": a_in, "out": a_out, "rec": a_rec, "order": bits, "start": 0},
+        {"in": b_in, "out": b_out, "rec": b_rec, "order": swapped, "start": 0},
+    ]
+    for one in streams:
+        one["rows"] = one["in"].shape[0]
+        one["base"] = 0
+        one["held"] = one["in"]
+        one["at"] = 0
+    for stage in range(stages):
+        flights = []
+        for one in streams:
+            bit = one["order"][stage]
+            half = one["rows"] // 2
+            mine = lax.div(place, bit) % 2
+            away = pl.multiple_of(one["at"] + (1 - mine) * half, 8)
+            landing = one["rec"].at[pl.ds(one["base"], half)]
+            flights.append(send_to(one["held"].at[pl.ds(away, half)], landing, target(bit)))
+            one["at"] = pl.multiple_of(one["at"] + mine * half, 8)
+            one["start"] = one["start"] + mine * half
+            one["rows"] = half
+        small = send_to(s_out, s_rec.at[stage], target(bits[stage]))
+        for one, copy in zip(streams, flights):
+            copy.wait()
+            half = one["rows"]
+            total = one["held"][pl.ds(one["at"], half)] + one["rec"][pl.ds(one["base"], half)]
+            if stage == stages - 1:
+                one["out"][pl.ds(pl.multiple_of(one["start"], 8), half)] = total
+            else:
+                one["rec"][pl.ds(one["base"], half)] = total
+            one["held"] = one["rec"]
+            one["at"] = one["base"]
+            one["base"] += half
+        small.wait()
+        s_out[...] = s_out[...] + s_rec[stage]
+    loss_row = lax.broadcasted_iota(jnp.int32, s_out.shape, 0) == s_out.shape[0] - 1
+    for stage in range(stages - 1, -1, -1):
+        flights = []
+        for one in streams:
+            bit = one["order"][stage]
+            mine = lax.div(place, bit) % 2
+            rows = one["rows"]
+            part = one["out"].at[pl.ds(pl.multiple_of(one["start"], 8), rows)]
+            flights.append(send_to(part, part, target(bit)))
+            one["start"] = one["start"] - mine * rows
+            one["rows"] = 2 * rows
+        behind = stages - 1 - stage
+        if behind < len(chan_bits):
+            small = send_to(
+                s_out, s_rec.at[stages + behind], {"chan": peer_of(lane, chan_bits[behind])}
+            )
+            small.wait()
+            s_out[...] = s_out[...] + jnp.where(loss_row, s_rec[stages + behind], 0.0)
+        for copy in flights:
+            copy.wait()
+
+
+def sum_over_patches(a, b, small):
+    count = lax.axis_size("patch")
+    chans = lax.axis_size("chan")
+    stages = len(bits_of(count))
+    chan_stages = len(bits_of(chans))
+    unit = 8 * count
+
+    def padded(rows):
+        return -(-rows // unit) * unit
+
+    a_rows, b_rows = padded(a.shape[0]), padded(b.shape[0])
+    a_full = jnp.pad(a, ((0, a_rows - a.shape[0]), (0, 0)))
+    b_full = jnp.pad(b, ((0, b_rows - b.shape[0]), (0, 0)))
+    copies = 5 * stages + chan_stages
+    spec = pl.BlockSpec(memory_space=pltpu.VMEM)
+
+    def kernel(*refs):
+        sum_kernel(count, chans, *refs)
+
+    a_sum, b_sum, s_sum = pl.pallas_call(
+        kernel,
+        out_shape=[
+            jax.ShapeDtypeStruct(a_full.shape, jnp.float32),
+            jax.ShapeDtypeStruct(b_full.shape, jnp.float32),
+            jax.ShapeDtypeStruct(small.shape, jnp.float32),
+        ],
+        in_specs=[spec] * 3,
+        out_specs=[spec] * 3,
+        scratch_shapes=[
+            pltpu.VMEM((a_rows - 8, a.shape[1]), jnp.float32),
+            pltpu.VMEM((b_rows - 8, b.shape[1]), jnp.float32),
+            pltpu.VMEM((stages + chan_stages,) + small.shape, jnp.float32),
+            pltpu.SemaphoreType.DMA((copies,)),
+            pltpu.SemaphoreType.DMA((copies,)),
+        ],
+        compiler_params=pltpu.CompilerParams(
+            collective_id=0, has_side_effects=True, vmem_limit_bytes=24 << 20
+        ),
+    )(a_full, b_full, small)
+    return a_sum[: a.shape[0]], b_sum[: b.shape[0]], s_sum
 
 
 def on_device(fields, w_one, bias_one, w_two, neighbour, seam_code, band_order, target, lat_weight):
@@ -160,21 +311,21 @@
             for tap in x_taps
         ]
     )
-    small_rows = -(-inner // chan_full) + 1
+    small_rows = -(-(inner // chan_full + 1) // 8) * 8
     small = jnp.concatenate(
         [
             jnp.pad(bias_local, (0, (small_rows - 1) * chan_full - inner)),
             jnp.pad(loss_local[None], (0, chan_full - 1)),
         ]
     ).reshape(small_rows, chan_full)
-    sum_two = lax.psum(two_local, "patch")
-    sums = lax.psum(
-        jnp.concatenate([one_local.reshape(9 * inner, chan_full), small], axis=0), "patch"
-    )
-    grad_one = sums[: 9 * inner].reshape(9, inner, chan_full)
-    grad_bias = sums[9 * inner : -1].reshape(-1)[:inner]
-    loss_value = sums[-1, 0] / (count * cells * chan_full)
-    return (loss_value, grad_one, sum_two, grad_bias)
+    sum_two, sum_one, sum_small = sum_over_patches(
+        two_local.reshape(9 * chan_full, inner), one_local.reshape(9 * inner, chan_full), small
+    )
+    grad_one = sum_one.reshape(9, inner, chan_full)
+    grad_two = sum_two.reshape(9, chan_full, inner)
+    grad_bias = sum_small[:-1].reshape(-1)[:inner]
+    loss_value = sum_small[-1, 0] / (count * cells * chan_full * chans)
+    return (loss_value, grad_one, grad_two, grad_bias)
 
 
 def solution(mesh):

time: 234 us -> 158 us (0.68)
  waiting for transfers between devices: 114 us -> 20.9 us
  Pallas kernels: 0 us -> 48.4 us
  between operations: 16.8 us -> 3.3 us
  local copies, waits for them, and re-layouts: 36.7 us -> 23.7 us
    psum x1 -> x0, waiting for transfers between devices: 101 us -> none  [on_device(): lax.psum(jnp.concatenate([one_local.reshape(9 * inner, chan_full), small]...]
    pallas_call x0 -> x1, Pallas kernels: none -> 48.4 us  [sum_over_patches(): pl.pallas_call(kernel, out_shape=[jax.ShapeDtypeStruct(a_full.shape, jnp....]
    conv_general_dilated x3, matrix products: 5.06 us -> 12 us  [conv(): lax.conv_general_dilated(values[None], weight, (1, 1), ((pad, pad), (pad,...]
    dot_general x9, matrix products: 9.39 us -> 2.49 us  [on_device(): lax.dot_general(grad_out, tap, (((0,), (0,)), ((), ())), preferred_elemen...]
    all_to_all x3, waiting for transfers between devices: 10.8 us -> 17 us  [swap(): lax.all_to_all(sent, 'patch', split_axis=0, concat_axis=0, tiled=True)]
    conv_general_dilated x13 -> x0, local copies, waits for them, and re-layouts: 6.06 us -> none  [conv(): lax.conv_general_dilated(values[None], weight, (1, 1), ((pad, pad), (pad,...]
    convert_element_type x2 -> x0, other arithmetic: 4.6 us -> none  [the longest x1 3.77 us: on_device(): pre_b = grad_pre.astype(jnp.bfloat16)]
    mul x3 -> x0, local copies, waits for them, and re-layouts: 4.44 us -> none  [smooth_gate(): return jax.nn.gelu(values, approximate=True)]
  transfers between devices with their start and end apart: 5 -> 4, of which waited for: 3 -> 4; matrix products, arithmetic and copies ran while one was open for 11% -> 9% of each run, Pallas kernels for 0% -> 0%
where the time goes in v2:
time: 158 us; the launch traced here: 157 us
  Pallas kernels  48.4 us (31%)
  local copies, waits for them, and re-layouts  23.7 us (15%)
  matrix products  21.7 us (14%)
  waiting for transfers between devices  20.9 us (13%)
  starting transfers between devices  16 us (10%)
  other arithmetic  13.3 us (8%)
  blocking collectives  9.91 us (6%)
  between operations  3.3 us (2%)
    pallas_call x1, Pallas kernels, sum_over_patches(): pl.pallas_call(kernel, out_shape=[jax.ShapeDtypeStruct(a_full.shape, jnp....  48.4 us
    all_to_all x3, waiting for transfers between devices, swap(): lax.all_to_all(sent, 'patch', split_axis=0, concat_axis=0, tiled=True)  17 us
    all_to_all x3, starting transfers between devices, swap(): lax.all_to_all(sent, 'patch', split_axis=0, concat_axis=0, tiled=True)  14.4 us
    conv_general_dilated x3, matrix products, conv(): lax.conv_general_dilated(values[None], weight, (1, 1), ((pad, pad), (pad,...  12 us
    unnamed x88, local copies, waits for them, and re-layouts  10.1 us
    all_gather x1, blocking collectives, on_device(): lax.all_gather(jnp.stack([fields[0], target[0]]), 'chan', axis=1, tiled=T...  9.91 us
    ppermute x1, waiting for transfers between devices, on_device(): lax.ppermute(rounded, 'chan', [(i, (i + shift) % chans) for i in range(ch...  3.93 us
  transfers between devices with their start and end apart: 4, of which 4 were waited for; matrix products, arithmetic and copies ran while one was open for 9% of the time, Pallas kernels for 0%

profile of v2, /device:TPU:0, one launch (start us, length us, event | category | flops | bytes accessed | tf_op | source)
XLA Modules:
  0.0 157.3 jit_solution(15215592935119684887)
XLA Ops:
  0.6 0.8 reduce.3
  1.5 1.1 copy.161
  2.6 1.1 copy.160
  3.7 0.6 pad_maximum_fusion.7
  4.3 9.9 %all_gather.3 = bf16[2,128,1024]{2,0,1:T(2,128)(2,1)S(1)} all-gather(bf16[2,64,1024]{2,0,1:T(2,128)(2,1)S(1)} %pad_maximum_fusion.7), channel_id=1, replica_groups=mesh['patch'=16,'chan'=2] {'chan'}, dimensions={1}, use_global_device_ids=true | all-gather | bytes 786432 | tf_op jit(solution)/shard_map/all_gather | solution.py:217
  14.2 0.7 fusion.89
  15.0 0.4 copy.208
  15.7 0.4 copy.205
  17.3 0.9 copy.168
  18.2 6.3 %all-to-all-start = ((bf16[16,97,128]{2,1,0:T(8,128)(2,1)}), bf16[16,97,128]{2,1,0:T(8,128)(2,1)S(1)}, u32[]{:S(2)}, u32[]{:S(2)}) async-start(bf16[16,97,128]{2,1,0:T(8,128)(2,1)} %copy.168), calls=%async_computation | async-start | bytes 851968 | tf_op jit(solution)/shard_map/all_to_all | solution.py:215
  24.6 0.6 gather_fusion
  25.2 0.6 iota_compare_fusion.5
  25.8 0.7 broadcast_select_fusion.3
  26.5 10.8 %all-to-all-done = bf16[16,97,128]{2,1,0:T(8,128)(2,1)S(1)} async-done(((bf16[16,97,128]{2,1,0:T(8,128)(2,1)}), bf16[16,97,128]{2,1,0:T(8,128)(2,1)S(1)}, u32[]{:S(2)}, u32[]{:S(2)}) %all-to-all-start) | async-done | bytes 397344 | tf_op jit(solution)/shard_map/all_to_all | solution.py:215
  37.9 3.6 %fusion.45 = f32[1,32,32,256]{3,0,2,1:T(1,128)S(1)} fusion(bf16[3,3,256,128]{3,2,1,0:T(8,128)(2,1)S(1)} %bitcast.310, bf16[1,34,34,128]{3,2,1,0:T(8,128)(2,1)S(1)} %maximum_bitcast_fusion.1), kind=kOutput, calls=%fused_computation.84 | convolution fusion | flops 603979776 | bytes 1934336 | tf_op jit(solution)/shard_map/conv_general_dilated | solution.py:25
  41.5 0.4 fusion.33
  41.8 0.7 fusion.88
  42.5 0.6 fusion.87
  43.1 1.0 copy.201
  44.4 0.9 pad_maximum_fusion.5
  45.3 0.7 reshape.556
  45.9 0.8 copy.264
  46.7 0.8 copy.265
  47.5 0.6 copy-done.21
  48.1 1.4 pad_maximum_fusion.9
  49.5 1.4 rev.14
  50.9 1.0 broadcast_select_fusion
  51.8 1.0 convolution_convert_fusion.2
  52.8 0.8 copy.177
  53.6 4.4 %all-to-all-start.1 = ((bf16[16,32,256]{2,1,0:T(8,128)(2,1)}), bf16[16,32,256]{2,1,0:T(8,128)(2,1)}, u32[]{:S(2)}, u32[]{:S(2)}) async-start(bf16[16,32,256]{2,1,0:T(8,128)(2,1)} %copy.177), calls=%async_computation.1 | async-start | bytes 524288 | tf_op jit(solution)/shard_map/all_to_all | solution.py:215
  58.0 1.1 fusion.91
  59.1 1.0 fusion.90
  60.1 0.5 copy-done.1
  60.6 1.1 fusion.41
  61.7 6.2 %all-to-all-done.1 = bf16[16,32,256]{2,1,0:T(8,128)(2,1)} async-done(((bf16[16,32,256]{2,1,0:T(8,128)(2,1)}), bf16[16,32,256]{2,1,0:T(8,128)(2,1)}, u32[]{:S(2)}, u32[]{:S(2)}) %all-to-all-start.1) | async-done | bytes 262176 | tf_op jit(solution)/shard_map/all_to_all | solution.py:215
  67.9 1.2 fusion.58
  69.2 0.4 maximum_bitcast_fusion
  69.7 0.5 pad_maximum_fusion
  70.1 1.1 pad_maximum_fusion.1
  71.2 3.9 %fusion = f32[1,32,32,128]{3,0,2,1:T(1,128)S(1)} fusion(bf16[3,3,128,256]{3,2,1,0:T(8,128)(2,1)S(1)} %bitcast.255, bf16[1,34,34,256]{3,2,1,0:T(8,128)(2,1)S(1)} %maximum_bitcast_fusion), kind=kOutput, calls=%fused_computation.8 | convolution fusion | flops 603979776 | bytes 1705984 | tf_op jit(solution)/shard_map/conv_general_dilated | solution.py:25
  75.2 1.5 collective-permute-start
  76.7 1.1 fusion.86
  77.9 1.5 fusion.85
  79.4 3.9 %collective-permute-done = bf16[1024,128]{1,0:T(8,128)(2,1)S(1)} collective-permute-done((bf16[1024,128]{1,0:T(8,128)(2,1)S(1)}, bf16[1024,128]{1,0:T(8,128)(2,1)S(1)}, u32[]{:S(2)}, u32[]{:S(2)}) %collective-permute-start) | collective-permute-done | bytes 262176 | tf_op jit(solution)/shard_map/ppermute | solution.py:247
  83.3 0.8 fusion.48
  84.9 0.7 copy.189
  85.6 3.7 %all-to-all-start.2 = ((bf16[16,32,128]{2,1,0:T(8,128)(2,1)}), bf16[16,32,128]{2,1,0:T(8,128)(2,1)S(1)}, u32[]{:S(2)}, u32[]{:S(2)}) async-start(bf16[16,32,128]{2,1,0:T(8,128)(2,1)} %copy.189), calls=%async_computation.2 | async-start | bytes 262144 | tf_op jit(solution)/shard_map/all_to_all | solution.py:215
  89.4 4.5 %fusion.49 = f32[1,32,32,256]{3,0,2,1:T(1,128)} fusion(bf16[3,3,128,256]{3,2,1,0:T(8,128)(2,1)S(1)} %bitcast.256, bf16[1,32,32,128]{3,2,1,0:T(8,128)(2,1)S(1)} %bitcast.272), kind=kOutput, calls=%fused_computation.91 | convolution fusion | flops 579076096 | bytes 1900544 | tf_op jit(solution)/shard_map/conv_general_dilated | solution.py:25
  94.5 0.4 copy-done.7
  97.4 0.4 convolution_convert_fusion
  98.2 1.6 %fusion.83 = (f32[256]{0:T(256)S(1)}, bf16[1,32,32,256]{3,2,1,0:T(8,128)(2,1)S(1)}) fusion(f32[256]{0:T(256)S(1)} %copy-done.29, f32[1,32,32,256]{3,0,2,1:T(1,128)S(1)} %fusion.45, f32[32,256]{1,0:T(8,128)S(1)} %get-tuple-element.49, pred[32]{0:T(512)(128)(4,1)S(1)} %copy-done.32, f32[32,256]{1,0:T(8,128)S(1)} %get-tuple-element.50, ...), kind=kLoop, calls=%fused_computation.173 | loop fusion | flops 7864064 | bytes 2754624 | tf_op jit(solution)/shard_map/reduce_sum | solution.py:299
  99.9 0.3 fusion.10
  100.3 0.3 fusion.9
  101.2 0.3 fusion.7
  101.5 0.3 fusion.6
  101.9 0.3 fusion.5
  102.6 0.3 fusion.3
  102.9 0.3 fusion.2
  103.3 0.7 fusion.70.refs_2_
  104.0 48.4 %shard_map.129 = (f32[1152,256]{1,0:T(8,128)S(1)}, f32[2304,128]{1,0:T(8,128)S(1)}, f32[8,128]{1,0:T(8,128)S(1)}) custom-call(f32[1152,256]{1,0:T(8,128)S(1)} %bitcast.258, f32[2304,128]{1,0:T(8,128)S(1)} %bitcast.259, f32[8,128]{1,0:T(8,128)S(1)} %fusion.70.refs_2_), custom_call_target="tpu_custom_call" | custom-call | tf_op jit(solution)/shard_map/pallas_call | solution.py:165
  152.4 0.5 slice.240
  152.9 0.6 slice_bitcast_fusion.8
  154.1 1.0 copy.289
  155.1 1.0 copy.290
  (138 shorter events, 7.4 us)
Async XLA Ops:
  0.6 70.6 %copy-start = (bf16[9,128,256]{2,1,0:T(8,128)(2,1)S(1)}, bf16[9,128,256]{2,1,0:T(8,128)(2,1)}, u32[]{:S(2)}) copy-start(bf16[9,128,256]{2,1,0:T(8,128)(2,1)} %param.13) | copy-start | bytes 1769476
  15.0 1.2 copy-start.31
  15.0 1.4 copy-start.34
  15.0 2.1 %copy-start.35 = (s32[16]{0:T(128)S(1)}, s32[16]{0:T(128)}, u32[]{:S(2)}) copy-start(s32[16]{0:T(128)} %param.16) | copy-start | bytes 196
  16.4 9.4 %copy-start.26 = (pred[4]{0:T(512)(128)(4,1)}, pred[4]{0:T(512)(128)(4,1)S(1)}, u32[]{:S(2)}) copy-start(pred[4]{0:T(512)(128)(4,1)S(1)} %compare_reduce_fusion) | copy-start | bytes 16
  16.7 20.6 %copy-start.23 = (s32[4]{0:T(128)}, s32[4]{0:T(128)S(1)}, u32[]{:S(2)}) copy-start(s32[4]{0:T(128)S(1)} %get-tuple-element.64) | copy-start | bytes 52
  17.3 7.3 %copy-start.22 = (s32[4,3]{1,0:T(4,128)S(1)}, s32[4,3]{1,0:T(4,128)}, u32[]{:S(2)}) copy-start(s32[4,3]{1,0:T(4,128)} %constant.54.clone) | copy-start | bytes 148
  18.2 19.7 %copy-start.36 = (bf16[9,256,128]{2,1,0:T(8,128)(2,1)S(1)}, bf16[9,256,128]{2,1,0:T(8,128)(2,1)}, u32[]{:S(2)}) copy-start(bf16[9,256,128]{2,1,0:T(8,128)(2,1)} %param.11) | copy-start | bytes 1769476
  18.2 19.1 %all-to-all-start = ((bf16[16,97,128]{2,1,0:T(8,128)(2,1)}), bf16[16,97,128]{2,1,0:T(8,128)(2,1)S(1)}, u32[]{:S(2)}, u32[]{:S(2)}) async-start(bf16[16,97,128]{2,1,0:T(8,128)(2,1)} %copy.168), calls=%async_computation | async-start | bytes 851968 | tf_op jit(solution)/shard_map/all_to_all | solution.py:215
  37.3 21.8 %copy-start.10 = (bf16[16,97,128]{2,1,0:T(8,128)(2,1)}, bf16[16,97,128]{2,1,0:T(8,128)(2,1)S(1)}, u32[]{:S(2)}) copy-start(bf16[16,97,128]{2,1,0:T(8,128)(2,1)S(1)} %all-to-all-done) | copy-start | bytes 1191940
  37.9 3.6 %copy-start.28 = (f32[256]{0:T(256)S(1)}, f32[256]{0:T(256)}, u32[]{:S(2)}) copy-start(f32[256]{0:T(256)} %param.12) | copy-start | bytes 3076
  46.7 0.8 copy-start.20
  47.5 0.6 copy-start.21
  53.6 14.3 %all-to-all-start.1 = ((bf16[16,32,256]{2,1,0:T(8,128)(2,1)}), bf16[16,32,256]{2,1,0:T(8,128)(2,1)}, u32[]{:S(2)}, u32[]{:S(2)}) async-start(bf16[16,32,256]{2,1,0:T(8,128)(2,1)} %copy.177), calls=%async_computation.1 | async-start | bytes 524288 | tf_op jit(solution)/shard_map/all_to_all | solution.py:215
  59.1 1.5 copy-start.1
  59.1 1.5 copy-start.29
  60.6 7.3 %copy-start.24 = (s32[4]{0:T(128)S(1)}, s32[4]{0:T(128)}, u32[]{:S(2)}) copy-start(s32[4]{0:T(128)} %copy-done.23) | copy-start | bytes 52
  75.2 8.1 %collective-permute-start = (bf16[1024,128]{1,0:T(8,128)(2,1)S(1)}, bf16[1024,128]{1,0:T(8,128)(2,1)S(1)}, u32[]{:S(2)}, u32[]{:S(2)}) collective-permute-start(bf16[1024,128]{1,0:T(8,128)(2,1)S(1)} %convert_element_type.102), channel_id=1, source_target_pairs={{0,1},{1,0},{2,3},{3,2},{4,5},{5,4},{6,7},{7,6},{8,9},{9,8},{10,11... | collective-permute-start | bytes 786440 | tf_op jit(solution)/shard_map/ppermute | solution.py:247
  77.8 5.5 %slice-start = ((bf16[16,97,128]{2,1,0:T(8,128)(2,1)}), bf16[16,64,128]{2,1,0:T(8,128)(2,1)S(1)}, s32[]{:S(2)}) async-start(bf16[16,97,128]{2,1,0:T(8,128)(2,1)} %copy-done.10), calls=%async_computation.3 | async-start | bytes 524288 | tf_op jit(solution)/shard_map/slice | solution.py:233
  77.8 5.5 %copy-start.25 = (f32[1024]{0:T(1024)S(1)}, f32[1024]{0:T(1024)}, u32[]{:S(2)}) copy-start(f32[1024]{0:T(1024)} %reshape.556) | copy-start | bytes 12292
  79.4 5.1 %copy-start.27 = (pred[4]{0:T(512)(128)(4,1)S(1)}, pred[4]{0:T(512)(128)(4,1)}, u32[]{:S(2)}) copy-start(pred[4]{0:T(512)(128)(4,1)} %copy-done.26) | copy-start | bytes 16
  85.6 11.4 %all-to-all-start.2 = ((bf16[16,32,128]{2,1,0:T(8,128)(2,1)}), bf16[16,32,128]{2,1,0:T(8,128)(2,1)S(1)}, u32[]{:S(2)}, u32[]{:S(2)}) async-start(bf16[16,32,128]{2,1,0:T(8,128)(2,1)} %copy.189), calls=%async_computation.2 | async-start | bytes 262144 | tf_op jit(solution)/shard_map/all_to_all | solution.py:215
  89.3 4.5 %copy-start.3 = (bf16[32,32,256]{2,1,0:T(8,128)(2,1)S(1)}, bf16[32,32,256]{2,1,0:T(8,128)(2,1)}, u32[]{:S(2)}) copy-start(bf16[32,32,256]{2,1,0:T(8,128)(2,1)} %get-tuple-element.23) | copy-start | bytes 1572868
  89.3 4.8 %copy-start.9 = (bf16[32,32,256]{2,1,0:T(8,128)(2,1)S(1)}, bf16[32,32,256]{2,1,0:T(8,128)(2,1)}, u32[]{:S(2)}) copy-start(bf16[32,32,256]{2,1,0:T(8,128)(2,1)} %get-tuple-element.16) | copy-start | bytes 1572868
  93.9 1.0 copy-start.7
  93.9 1.3 copy-start.4
  94.2 1.3 copy-start.8
  94.9 1.1 copy-start.6
  95.2 1.1 copy-start.2
  95.5 1.1 copy-start.5
  96.3 1.0 copy-start.30
  96.9 1.1 copy-start.32
  96.9 1.1 copy-start.33
  97.0 1.2 copy-start.13
  98.2 1.6 %copy-start.18 = (bf16[32,32,128]{2,1,0:T(8,128)(2,1)S(1)}, bf16[32,32,128]{2,1,0:T(8,128)(2,1)}, u32[]{:S(2)}) copy-start(bf16[32,32,128]{2,1,0:T(8,128)(2,1)} %get-tuple-element.35) | copy-start | bytes 786436
  98.2 2.0 %copy-start.12 = (bf16[32,32,128]{2,1,0:T(8,128)(2,1)S(1)}, bf16[32,32,128]{2,1,0:T(8,128)(2,1)}, u32[]{:S(2)}) copy-start(bf16[32,32,128]{2,1,0:T(8,128)(2,1)} %get-tuple-element.39) | copy-start | bytes 786436
  99.9 1.0 copy-start.19
  99.9 1.3 copy-start.16
  100.8 1.1 copy-start.17
  101.2 1.1 copy-start.14
  101.5 1.1 copy-start.11
  101.9 1.1 copy-start.15

commit v3 on v2

--- a/solution.py
+++ b/solution.py
@@ -85,62 +85,73 @@
         copy.start()
         return copy
 
+    def split(rows):
+        units = rows // (8 * count)
+        first = (units - units // 2) * 8 * count
+        return [(0, first), (first, rows - first)] if units > 1 else [(0, rows)]
+
     s_out[...] = s_in[...]
-    streams = [
-        {"in": a_in, "out": a_out, "rec": a_rec, "order": bits, "start": 0},
-        {"in": b_in, "out": b_out, "rec": b_rec, "order": swapped, "start": 0},
+    groups = [
+        [
+            {"in": held, "out": out, "rec": rec, "order": order, "start": low, "rows": rows,
+             "base": low, "held": held, "at": low}
+            for low, rows in split(held.shape[0])
+        ]
+        for held, out, rec, order in ((a_in, a_out, a_rec, bits), (b_in, b_out, b_rec, swapped))
     ]
+    streams = groups[0][:1] + groups[1][:1] + groups[0][1:] + groups[1][1:]
+
+    def scatter(one, stage):
+        bit = one["order"][stage]
+        half = one["rows"] // 2
+        mine = lax.div(place, bit) % 2
+        away = pl.multiple_of(one["at"] + (1 - mine) * half, 8)
+        landing = one["rec"].at[pl.ds(one["base"], half)]
+        one["copy"] = send_to(one["held"].at[pl.ds(away, half)], landing, target(bit))
+        one["at"] = pl.multiple_of(one["at"] + mine * half, 8)
+        one["start"] = one["start"] + mine * half
+        one["rows"] = half
+
+    def gather(one, stage):
+        rows = one["rows"]
+        bit = one["order"][stage]
+        mine = lax.div(place, bit) % 2
+        part = one["out"].at[pl.ds(pl.multiple_of(one["start"], 8), rows)]
+        one["copy"] = send_to(part, part, target(bit))
+        one["start"] = one["start"] - mine * rows
+        one["rows"] = 2 * rows
+
     for one in streams:
-        one["rows"] = one["in"].shape[0]
-        one["base"] = 0
-        one["held"] = one["in"]
-        one["at"] = 0
+        scatter(one, 0)
+    small = send_to(s_out, s_rec.at[0], target(bits[0]))
     for stage in range(stages):
-        flights = []
         for one in streams:
-            bit = one["order"][stage]
-            half = one["rows"] // 2
-            mine = lax.div(place, bit) % 2
-            away = pl.multiple_of(one["at"] + (1 - mine) * half, 8)
-            landing = one["rec"].at[pl.ds(one["base"], half)]
-            flights.append(send_to(one["held"].at[pl.ds(away, half)], landing, target(bit)))
-            one["at"] = pl.multiple_of(one["at"] + mine * half, 8)
-            one["start"] = one["start"] + mine * half
-            one["rows"] = half
-        small = send_to(s_out, s_rec.at[stage], target(bits[stage]))
-        for one, copy in zip(streams, flights):
-            copy.wait()
+            one["copy"].wait()
             half = one["rows"]
             total = one["held"][pl.ds(one["at"], half)] + one["rec"][pl.ds(one["base"], half)]
             if stage == stages - 1:
                 one["out"][pl.ds(pl.multiple_of(one["start"], 8), half)] = total
+                gather(one, stage)
             else:
                 one["rec"][pl.ds(one["base"], half)] = total
-            one["held"] = one["rec"]
-            one["at"] = one["base"]
-            one["base"] += half
+                one["held"] = one["rec"]
+                one["at"] = one["base"]
+                one["base"] += half
+                scatter(one, stage + 1)
         small.wait()
         s_out[...] = s_out[...] + s_rec[stage]
+        if stage + 1 < stages:
+            small = send_to(s_out, s_rec.at[stage + 1], target(bits[stage + 1]))
     loss_row = lax.broadcasted_iota(jnp.int32, s_out.shape, 0) == s_out.shape[0] - 1
+    for place_at, bit in enumerate(chan_bits):
+        small = send_to(s_out, s_rec.at[stages + place_at], {"chan": peer_of(lane, bit)})
+        small.wait()
+        s_out[...] = s_out[...] + jnp.where(loss_row, s_rec[stages + place_at], 0.0)
     for stage in range(stages - 1, -1, -1):
-        flights = []
         for one in streams:
-            bit = one["order"][stage]
-            mine = lax.div(place, bit) % 2
-            rows = one["rows"]
-            part = one["out"].at[pl.ds(pl.multiple_of(one["start"], 8), rows)]
-            flights.append(send_to(part, part, target(bit)))
-            one["start"] = one["start"] - mine * rows
-            one["rows"] = 2 * rows
-        behind = stages - 1 - stage
-        if behind < len(chan_bits):
-            small = send_to(
-                s_out, s_rec.at[stages + behind], {"chan": peer_of(lane, chan_bits[behind])}
-            )
-            small.wait()
-            s_out[...] = s_out[...] + jnp.where(loss_row, s_rec[stages + behind], 0.0)
-        for copy in flights:
-            copy.wait()
+            one["copy"].wait()
+            if stage > 0:
+                gather(one, stage - 1)
 
 
 def sum_over_patches(a, b, small):
@@ -156,7 +167,7 @@
     a_rows, b_rows = padded(a.shape[0]), padded(b.shape[0])
     a_full = jnp.pad(a, ((0, a_rows - a.shape[0]), (0, 0)))
     b_full = jnp.pad(b, ((0, b_rows - b.shape[0]), (0, 0)))
-    copies = 5 * stages + chan_stages
+    copies = 9 * stages + chan_stages
     spec = pl.BlockSpec(memory_space=pltpu.VMEM)
 
     def kernel(*refs):
@@ -172,8 +183,8 @@
         in_specs=[spec] * 3,
         out_specs=[spec] * 3,
         scratch_shapes=[
-            pltpu.VMEM((a_rows - 8, a.shape[1]), jnp.float32),
-            pltpu.VMEM((b_rows - 8, b.shape[1]), jnp.float32),
+            pltpu.VMEM((a_rows, a.shape[1]), jnp.float32),
+            pltpu.VMEM((b_rows, b.shape[1]), jnp.float32),
             pltpu.VMEM((stages + chan_stages,) + small.shape, jnp.float32),
             pltpu.SemaphoreType.DMA((copies,)),
             pltpu.SemaphoreType.DMA((copies,)),
@@ -228,11 +239,13 @@
     band_parts = jnp.einsum(
         "ps,skc->pkc", slots, band_parts, preferred_element_type=jnp.float32
     ).astype(jnp.bfloat16)
-    first = swap(jnp.concatenate([to_send(x_grid), band_parts], axis=1))
-    x_pad = with_frame(x_grid, picked(first[:, :length]))
-    target_patch = first[:, length : length + part].reshape(cells, chan_full)
+    first = swap(to_send(x_grid))
+    band_parts, first = lax.optimization_barrier((band_parts, first))
+    second = swap(band_parts)
+    x_pad = with_frame(x_grid, picked(first))
+    target_patch = second[:, :part].reshape(cells, chan_full)
     lat_w = (
-        first[:, length + part :].reshape(count, lat_rows * chan_full)[:, :part].reshape(cells, 1)
+        second[:, part:].reshape(count, lat_rows * chan_full)[:, :part].reshape(cells, 1)
     ).astype(jnp.float32)
 
     preact = conv(x_pad, w_one.reshape(3, 3, inner, chan_full), 0, "HWOI") + bias_one

time: 158 us -> 144 us (0.911)
  Pallas kernels: 48.4 us -> 42.9 us
  waiting for transfers between devices: 20.9 us -> 15.9 us
  starting transfers between devices: 16 us -> 20.8 us
  local copies, waits for them, and re-layouts: 23.7 us -> 19.2 us
  other arithmetic: 13.3 us -> 9.96 us
    pallas_call x1, Pallas kernels: 48.4 us -> 42.9 us  [sum_over_patches(): pl.pallas_call(kernel, out_shape=[jax.ShapeDtypeStruct(a_full.shape, jnp....]
    all_to_all x3 -> x4, starting transfers between devices: 14.4 us -> 19.3 us  [swap(): lax.all_to_all(sent, 'patch', split_axis=0, concat_axis=0, tiled=True)]
    all_to_all x3 -> x4, waiting for transfers between devices: 17 us -> 12.9 us  [swap(): lax.all_to_all(sent, 'patch', split_axis=0, concat_axis=0, tiled=True)]
    unnamed x88 -> x67, local copies, waits for them, and re-layouts: 10.1 us -> 8.01 us
  transfers between devices with their start and end apart: 4 -> 5, of which waited for: 4 -> 4; matrix products, arithmetic and copies ran while one was open for 9% -> 14% of each run, Pallas kernels for 0% -> 0%
where the time goes in v3:
time: 144 us; the launch traced here: 143 us
  Pallas kernels  42.9 us (30%)
  matrix products  21.2 us (15%)
  starting transfers between devices  20.8 us (14%)
  local copies, waits for them, and re-layouts  19.2 us (13%)
  waiting for transfers between devices  15.9 us (11%)
  other arithmetic  9.96 us (7%)
  blocking collectives  9.91 us (7%)
  between operations  3.25 us (2%)
    pallas_call x1, Pallas kernels, sum_over_patches(): pl.pallas_call(kernel, out_shape=[jax.ShapeDtypeStruct(a_full.shape, jnp....  42.9 us
    all_to_all x4, starting transfers between devices, swap(): lax.all_to_all(sent, 'patch', split_axis=0, concat_axis=0, tiled=True)  19.3 us
    all_to_all x4, waiting for transfers between devices, swap(): lax.all_to_all(sent, 'patch', split_axis=0, concat_axis=0, tiled=True)  12.9 us
    conv_general_dilated x3, matrix products, conv(): lax.conv_general_dilated(values[None], weight, (1, 1), ((pad, pad), (pad,...  12 us
    all_gather x1, blocking collectives, on_device(): lax.all_gather(jnp.stack([fields[0], target[0]]), 'chan', axis=1, tiled=T...  9.91 us
    unnamed x67, local copies, waits for them, and re-layouts  8.01 us
    dot_general x9, matrix products, on_device(): lax.dot_general(grad_out, tap, (((0,), (0,)), ((), ())), preferred_elemen...  3.53 us
    dot_general x9, matrix products, on_device(): lax.dot_general(pre_b, tap, (((0,), (0,)), ((), ())), preferred_element_t...  3.03 us
  transfers between devices with their start and end apart: 5, of which 4 were waited for; matrix products, arithmetic and copies ran while one was open for 14% of the time, Pallas kernels for 0%

profile of v3, /device:TPU:0, one launch (start us, length us, event | category | flops | bytes accessed | tf_op | source)
XLA Modules:
  0.0 143.1 jit_solution(8065330453255464797)
XLA Ops:
  0.6 1.2 copy.172
  1.8 1.1 copy.171
  2.9 0.6 pad_maximum_fusion.6
  3.5 9.9 %all_gather.3 = bf16[2,128,1024]{2,0,1:T(2,128)(2,1)S(1)} all-gather(bf16[2,64,1024]{2,0,1:T(2,128)(2,1)S(1)} %pad_maximum_fusion.6), channel_id=1, replica_groups=mesh['patch'=16,'chan'=2] {'chan'}, dimensions={1}, use_global_device_ids=true | all-gather | bytes 786432 | tf_op jit(solution)/shard_map/all_gather | solution.py:228
  13.5 0.7 fusion.89
  14.2 0.4 copy.218
  15.3 0.3 convolution_convert_fusion.4
  15.6 0.7 copy.177
  16.3 6.2 %all-to-all-start = ((bf16[16,32,128]{2,1,0:T(8,128)(2,1)}), bf16[16,32,128]{2,1,0:T(8,128)(2,1)S(1)}, u32[]{:S(2)}, u32[]{:S(2)}) async-start(bf16[16,32,128]{2,1,0:T(8,128)(2,1)} %copy.177), calls=%async_computation | async-start | bytes 262144 | tf_op jit(solution)/shard_map/all_to_all | solution.py:226
  22.7 0.6 gather_fusion
  23.4 0.4 copy.217
  24.3 6.2 %all-to-all-done = bf16[16,32,128]{2,1,0:T(8,128)(2,1)S(1)} async-done(((bf16[16,32,128]{2,1,0:T(8,128)(2,1)}), bf16[16,32,128]{2,1,0:T(8,128)(2,1)S(1)}, u32[]{:S(2)}, u32[]{:S(2)}) %all-to-all-start) | async-done | bytes 131104 | tf_op jit(solution)/shard_map/all_to_all | solution.py:226
  31.0 3.6 %fusion.45 = f32[1,32,32,256]{3,0,2,1:T(1,128)S(1)} fusion(bf16[3,3,256,128]{3,2,1,0:T(8,128)(2,1)S(1)} %bitcast.310, bf16[1,34,34,128]{3,2,1,0:T(8,128)(2,1)S(1)} %maximum_bitcast_fusion.1), kind=kOutput, calls=%fused_computation.84 | convolution fusion | flops 603979776 | bytes 1934336 | tf_op jit(solution)/shard_map/conv_general_dilated | solution.py:25
  34.6 0.4 fusion.33
  35.1 1.0 copy.213
  36.3 0.8 pad_maximum_fusion.4
  37.2 0.8 copy.178
  38.2 0.4 convolution_convert_fusion.2
  38.5 0.8 copy.187
  39.3 3.5 %all-to-all-start.2 = ((bf16[16,32,256]{2,1,0:T(8,128)(2,1)}), bf16[16,32,256]{2,1,0:T(8,128)(2,1)S(1)}, u32[]{:S(2)}, u32[]{:S(2)}) async-start(bf16[16,32,256]{2,1,0:T(8,128)(2,1)} %copy.187), calls=%async_computation.2 | async-start | bytes 524288 | tf_op jit(solution)/shard_map/all_to_all | solution.py:226
  42.9 1.0 fusion.91
  43.9 1.0 fusion.90
  44.8 0.5 copy-done.1
  45.4 1.1 fusion.41
  46.5 6.3 %all-to-all-done.2 = bf16[16,32,256]{2,1,0:T(8,128)(2,1)S(1)} async-done(((bf16[16,32,256]{2,1,0:T(8,128)(2,1)}), bf16[16,32,256]{2,1,0:T(8,128)(2,1)S(1)}, u32[]{:S(2)}, u32[]{:S(2)}) %all-to-all-start.2) | async-done | bytes 262176 | tf_op jit(solution)/shard_map/all_to_all | solution.py:226
  52.9 3.7 %all-to-all-start.1 = ((bf16[16,65,128]{2,1,0:T(8,128)(2,1)}), bf16[16,65,128]{2,1,0:T(8,128)(2,1)S(1)}, u32[]{:S(2)}, u32[]{:S(2)}) async-start(bf16[16,65,128]{2,1,0:T(8,128)(2,1)} %copy.178), calls=%async_computation.1 | async-start | bytes 589824 | tf_op jit(solution)/shard_map/all_to_all | solution.py:226
  57.0 0.4 maximum_bitcast_fusion
  57.4 0.4 pad_maximum_fusion
  57.9 3.9 %fusion = f32[1,32,32,128]{3,0,2,1:T(1,128)S(1)} fusion(bf16[3,3,128,256]{3,2,1,0:T(8,128)(2,1)S(1)} %bitcast.255, bf16[1,34,34,256]{3,2,1,0:T(8,128)(2,1)S(1)} %maximum_bitcast_fusion), kind=kOutput, calls=%fused_computation.8 | convolution fusion | flops 603979776 | bytes 1705984 | tf_op jit(solution)/shard_map/conv_general_dilated | solution.py:25
  61.8 1.6 %collective-permute-start = (bf16[1024,128]{1,0:T(8,128)(2,1)S(1)}, bf16[1024,128]{1,0:T(8,128)(2,1)}, u32[]{:S(2)}, u32[]{:S(2)}) collective-permute-start(bf16[1024,128]{1,0:T(8,128)(2,1)S(1)} %convert_element_type.102), channel_id=1, source_target_pairs={{0,1},{1,0},{2,3},{3,2},{4,5},{5,4},{6,7},{7,6},{8,9},{9,8},{10,11... | collective-permute-start | bytes 786440 | tf_op jit(solution)/shard_map/ppermute | solution.py:260
  63.4 1.2 fusion.86
  64.6 1.5 %fusion.85 = (bf16[32,32,256]{2,1,0:T(8,128)(2,1)}, bf16[32,32,256]{2,1,0:T(8,128)(2,1)}, bf16[32,32,256]{2,1,0:T(8,128)(2,1)}) fusion(bf16[34,33,256]{2,1,0:T(8,128)(2,1)S(1)} %get-tuple-element.24), kind=kLoop, calls=%fused_computation.173 | loop fusion | bytes 3145728 | tf_op jit(solution)/shard_map/slice | solution.py:272
  66.1 1.0 pad_maximum_fusion.1
  67.3 3.0 %collective-permute-done = bf16[1024,128]{1,0:T(8,128)(2,1)} collective-permute-done((bf16[1024,128]{1,0:T(8,128)(2,1)S(1)}, bf16[1024,128]{1,0:T(8,128)(2,1)}, u32[]{:S(2)}, u32[]{:S(2)}) %collective-permute-start) | collective-permute-done | bytes 262176 | tf_op jit(solution)/shard_map/ppermute | solution.py:260
  70.3 1.8 %fusion.48 = (f32[]{:T(128)}, bf16[1024,128]{1,0:T(8,128)(2,1)S(1)}) fusion(f32[1024]{0:T(1024)S(1)} %reshape.556, bf16[16,64,128]{2,1,0:T(8,128)(2,1)S(1)} %slice.261, f32[1024,128]{1,0:T(8,128)S(1)} %bitcast.287, bf16[1024,128]{1,0:T(8,128)(2,1)} %collective-permute-done, bf16[1,128,1024]{1,2,0:T(8,128)(2,1)S(1)} %copy.218), kind=kLoop, calls=%fused_computation.87 | loop fusion | flops 1441791 | bytes 1576964 | tf_op jit(solution)/shard_map/reduce_sum | solution.py:266
  72.1 1.3 fusion.19
  73.6 0.3 convolution_convert_fusion.3
  73.9 0.7 copy.199
  74.6 5.8 %all-to-all-start.3 = ((bf16[16,32,128]{2,1,0:T(8,128)(2,1)}), bf16[16,32,128]{2,1,0:T(8,128)(2,1)S(1)}, u32[]{:S(2)}, u32[]{:S(2)}) async-start(bf16[16,32,128]{2,1,0:T(8,128)(2,1)} %copy.199), calls=%async_computation.3 | async-start | bytes 262144 | tf_op jit(solution)/shard_map/all_to_all | solution.py:226
  80.5 4.5 %fusion.49 = f32[1,32,32,256]{3,0,2,1:T(1,128)} fusion(bf16[3,3,128,256]{3,2,1,0:T(8,128)(2,1)S(1)} %bitcast.256, bf16[1,32,32,128]{3,2,1,0:T(8,128)(2,1)S(1)} %bitcast.272), kind=kOutput, calls=%fused_computation.91 | convolution fusion | flops 579076096 | bytes 1900544 | tf_op jit(solution)/shard_map/conv_general_dilated | solution.py:25
  85.0 0.3 fusion.18
  85.3 0.3 fusion.17
  85.6 0.4 copy-done.7
  86.3 0.3 fusion.15
  86.7 0.3 fusion.14
  87.5 0.3 fusion.12
  88.1 0.3 all-to-all-done.3
  88.7 0.4 convolution_convert_fusion
  89.6 1.6 %fusion.83 = (f32[256]{0:T(256)S(1)}, bf16[1,32,32,256]{3,2,1,0:T(8,128)(2,1)S(1)}) fusion(f32[256]{0:T(256)S(1)} %copy-done.20, f32[1,32,32,256]{3,0,2,1:T(1,128)S(1)} %fusion.45, f32[32,256]{1,0:T(8,128)S(1)} %get-tuple-element.53, pred[32]{0:T(512)(128)(4,1)S(1)} %get-tuple-element.70, f32[32,256]{1,0:T(8,128)S(1)} %get-tuple-element.54, ...), kind=kLoop, calls=%fused_computation.172 | loop fusion | flops 7864064 | bytes 2754624 | tf_op jit(solution)/shard_map/reduce_sum | solution.py:312
  91.3 0.3 fusion.10
  91.6 0.3 fusion.9
  92.2 0.3 fusion.8
  92.6 0.3 fusion.7
  92.9 0.3 fusion.6
  93.3 0.3 fusion.5
  93.6 0.3 fusion.4
  94.0 0.3 fusion.3
  94.3 0.3 fusion.2
  94.7 0.7 fusion.70.refs_2_
  95.3 42.9 %shard_map.129 = (f32[1152,256]{1,0:T(8,128)S(1)}, f32[2304,128]{1,0:T(8,128)S(1)}, f32[8,128]{1,0:T(8,128)S(1)}) custom-call(f32[1152,256]{1,0:T(8,128)S(1)} %bitcast.258, f32[2304,128]{1,0:T(8,128)S(1)} %bitcast.259, f32[8,128]{1,0:T(8,128)S(1)} %fusion.70.refs_2_), custom_call_target="tpu_custom_call" | custom-call | tf_op jit(solution)/shard_map/pallas_call | solution.py:176
  138.2 0.5 slice.236
  138.7 0.6 slice_bitcast_fusion.8
  140.0 1.0 copy.298
  141.0 1.0 copy.299
  (116 shorter events, 5.1 us)
Async XLA Ops:
  0.6 57.2 %copy-start = (bf16[9,128,256]{2,1,0:T(8,128)(2,1)S(1)}, bf16[9,128,256]{2,1,0:T(8,128)(2,1)}, u32[]{:S(2)}) copy-start(bf16[9,128,256]{2,1,0:T(8,128)(2,1)} %param.13) | copy-start | bytes 1769476
  13.4 1.3 copy-start.21
  13.5 1.5 %copy-start.23 = (s32[16,4]{0,1:T(4,128)S(1)}, s32[16,4]{0,1:T(4,128)}, u32[]{:S(2)}) copy-start(s32[16,4]{0,1:T(4,128)} %param.14) | copy-start | bytes 772
  14.2 8.3 %copy-start.22 = (bf16[1,1024]{1,0:T(2,128)(2,1)S(1)}, bf16[1,1024]{1,0:T(2,128)(2,1)}, u32[]{:S(2)}) copy-start(bf16[1,1024]{1,0:T(2,128)(2,1)} %param.18) | copy-start | bytes 6148
  14.2 8.5 %copy-start.19 = (s32[4,3]{1,0:T(4,128)S(1)}, s32[4,3]{1,0:T(4,128)}, u32[]{:S(2)}) copy-start(s32[4,3]{1,0:T(4,128)} %constant.54.clone) | copy-start | bytes 148
  14.7 9.3 %copy-start.24 = (s32[16]{0:T(128)S(1)}, s32[16]{0:T(128)}, u32[]{:S(2)}) copy-start(s32[16]{0:T(128)} %param.16) | copy-start | bytes 196
  16.3 14.1 %all-to-all-start = ((bf16[16,32,128]{2,1,0:T(8,128)(2,1)}), bf16[16,32,128]{2,1,0:T(8,128)(2,1)S(1)}, u32[]{:S(2)}, u32[]{:S(2)}) async-start(bf16[16,32,128]{2,1,0:T(8,128)(2,1)} %copy.177), calls=%async_computation | async-start | bytes 262144 | tf_op jit(solution)/shard_map/all_to_all | solution.py:226
  23.8 7.2 %copy-start.25 = (bf16[9,256,128]{2,1,0:T(8,128)(2,1)S(1)}, bf16[9,256,128]{2,1,0:T(8,128)(2,1)}, u32[]{:S(2)}) copy-start(bf16[9,256,128]{2,1,0:T(8,128)(2,1)} %param.11) | copy-start | bytes 1769476
  31.0 3.6 %copy-start.20 = (f32[256]{0:T(256)S(1)}, f32[256]{0:T(256)}, u32[]{:S(2)}) copy-start(f32[256]{0:T(256)} %param.12) | copy-start | bytes 3076
  39.3 13.5 %all-to-all-start.2 = ((bf16[16,32,256]{2,1,0:T(8,128)(2,1)}), bf16[16,32,256]{2,1,0:T(8,128)(2,1)S(1)}, u32[]{:S(2)}, u32[]{:S(2)}) async-start(bf16[16,32,256]{2,1,0:T(8,128)(2,1)} %copy.187), calls=%async_computation.2 | async-start | bytes 524288 | tf_op jit(solution)/shard_map/all_to_all | solution.py:226
  43.9 1.5 %copy-start.1 = (f32[1,32,32,256]{3,2,0,1:T(8,128)S(1)}, f32[1,32,32,256]{3,2,0,1:T(8,128)}, u32[]{:S(2)}) copy-start(f32[1,32,32,256]{3,2,0,1:T(8,128)} %copy.213) | copy-start | bytes 3145732
  52.9 14.3 %all-to-all-start.1 = ((bf16[16,65,128]{2,1,0:T(8,128)(2,1)}), bf16[16,65,128]{2,1,0:T(8,128)(2,1)S(1)}, u32[]{:S(2)}, u32[]{:S(2)}) async-start(bf16[16,65,128]{2,1,0:T(8,128)(2,1)} %copy.178), calls=%async_computation.1 | async-start | bytes 589824 | tf_op jit(solution)/shard_map/all_to_all | solution.py:226
  61.8 8.5 %collective-permute-start = (bf16[1024,128]{1,0:T(8,128)(2,1)S(1)}, bf16[1024,128]{1,0:T(8,128)(2,1)}, u32[]{:S(2)}, u32[]{:S(2)}) collective-permute-start(bf16[1024,128]{1,0:T(8,128)(2,1)S(1)} %convert_element_type.102), channel_id=1, source_target_pairs={{0,1},{1,0},{2,3},{3,2},{4,5},{5,4},{6,7},{7,6},{8,9},{9,8},{10,11... | collective-permute-start | bytes 786440 | tf_op jit(solution)/shard_map/ppermute | solution.py:260
  74.6 13.8 %all-to-all-start.3 = ((bf16[16,32,128]{2,1,0:T(8,128)(2,1)}), bf16[16,32,128]{2,1,0:T(8,128)(2,1)S(1)}, u32[]{:S(2)}, u32[]{:S(2)}) async-start(bf16[16,32,128]{2,1,0:T(8,128)(2,1)} %copy.199), calls=%async_computation.3 | async-start | bytes 262144 | tf_op jit(solution)/shard_map/all_to_all | solution.py:226
  80.5 4.5 %copy-start.3 = (bf16[32,32,256]{2,1,0:T(8,128)(2,1)S(1)}, bf16[32,32,256]{2,1,0:T(8,128)(2,1)}, u32[]{:S(2)}) copy-start(bf16[32,32,256]{2,1,0:T(8,128)(2,1)} %get-tuple-element.27) | copy-start | bytes 1572868
  80.5 4.8 %copy-start.9 = (bf16[32,32,256]{2,1,0:T(8,128)(2,1)S(1)}, bf16[32,32,256]{2,1,0:T(8,128)(2,1)}, u32[]{:S(2)}) copy-start(bf16[32,32,256]{2,1,0:T(8,128)(2,1)} %get-tuple-element.20) | copy-start | bytes 1572868
  85.0 1.0 copy-start.7
  85.0 1.3 copy-start.4
  85.3 1.3 copy-start.8
  86.0 1.1 copy-start.6
  86.3 1.1 copy-start.2
  86.6 1.1 copy-start.5
  88.4 1.2 copy-start.12
  89.6 1.6 %copy-start.17 = (bf16[32,32,128]{2,1,0:T(8,128)(2,1)S(1)}, bf16[32,32,128]{2,1,0:T(8,128)(2,1)}, u32[]{:S(2)}) copy-start(bf16[32,32,128]{2,1,0:T(8,128)(2,1)} %get-tuple-element.39) | copy-start | bytes 786436
  89.6 2.0 %copy-start.11 = (bf16[32,32,128]{2,1,0:T(8,128)(2,1)S(1)}, bf16[32,32,128]{2,1,0:T(8,128)(2,1)}, u32[]{:S(2)}) copy-start(bf16[32,32,128]{2,1,0:T(8,128)(2,1)} %get-tuple-element.43) | copy-start | bytes 786436
  91.2 1.0 copy-start.18
  91.3 1.3 copy-start.15
  92.2 1.1 copy-start.16
  92.5 1.1 copy-start.14
  92.9 1.1 copy-start.10
  93.3 1.1 copy-start.13

commit v4 on v3

--- a/solution.py
+++ b/solution.py
@@ -225,17 +225,16 @@
     def swap(sent):
         return lax.all_to_all(sent, "patch", split_axis=0, concat_axis=0, tiled=True)
 
-    both = lax.all_gather(jnp.stack([fields[0], target[0]]), "chan", axis=1, tiled=True)
-    chan_full = both.shape[1]
-    x_grid = both[0].T.reshape(length, length, chan_full)
+    whole = lax.all_gather(fields[0], "chan", axis=0, tiled=True)
+    chan_full = whole.shape[0]
+    chan_own = fields.shape[1]
+    x_grid = whole.T.reshape(length, length, chan_full)
     slots = (band_order[None, :] == ids[:, None]).astype(jnp.bfloat16)
-    lat_rows = -(-part // chan_full)
+    lat_rows = -(-part // chan_own)
     lat_parts = jnp.pad(
-        lat_weight.reshape(count, part), ((0, 0), (0, lat_rows * chan_full - part))
-    ).reshape(count, lat_rows, chan_full)
-    band_parts = jnp.concatenate(
-        [both[1].T.reshape(count, part, chan_full), lat_parts], axis=1
-    )
+        lat_weight.reshape(count, part), ((0, 0), (0, lat_rows * chan_own - part))
+    ).reshape(count, lat_rows, chan_own)
+    band_parts = jnp.concatenate([target[0].T.reshape(count, part, chan_own), lat_parts], axis=1)
     band_parts = jnp.einsum(
         "ps,skc->pkc", slots, band_parts, preferred_element_type=jnp.float32
     ).astype(jnp.bfloat16)
@@ -243,9 +242,17 @@
     band_parts, first = lax.optimization_barrier((band_parts, first))
     second = swap(band_parts)
     x_pad = with_frame(x_grid, picked(first))
-    target_patch = second[:, :part].reshape(cells, chan_full)
+    lane = lax.axis_index("chan")
+    pieces = [second[:, :part].reshape(cells, chan_own)]
+    for shift in range(1, chans):
+        pieces.append(
+            lax.ppermute(pieces[0], "chan", [(i, (i + shift) % chans) for i in range(chans)])
+        )
+    target_patch = jnp.concatenate(
+        [lax.select_n((lane - c + chans) % chans, *pieces) for c in range(chans)], axis=1
+    )
     lat_w = (
-        second[:, part:].reshape(count, lat_rows * chan_full)[:, :part].reshape(cells, 1)
+        second[:, part:].reshape(count, lat_rows * chan_own)[:, :part].reshape(cells, 1)
     ).astype(jnp.float32)
 
     preact = conv(x_pad, w_one.reshape(3, 3, inner, chan_full), 0, "HWOI") + bias_one

time: 144 us -> 150 us (1.042)
  waiting for transfers between devices: 15.9 us -> 19 us
  other arithmetic: 9.96 us -> 12.8 us
  blocking collectives: 9.91 us -> 7.5 us
  local copies, waits for them, and re-layouts: 19.2 us -> 21.4 us
  starting transfers between devices: 20.8 us -> 23 us
    ppermute x0 -> x1, waiting for transfers between devices: none -> 3.55 us  [on_device(): lax.ppermute(pieces[0], 'chan', [(i, (i + shift) % chans) for i in range(...]
    convert_element_type x1 -> x2, other arithmetic: 0.01 us -> 3.17 us  [the longest x1 1.89 us: on_device(): pre_b = grad_pre.astype(jnp.bfloat16)]
    broadcast_in_dim x0 -> x8, local copies, waits for them, and re-layouts: none -> 2.82 us  [the longest x2 0.76 us: on_device(): jnp.where(row == 0, back[0][None], 0.0)]
    all_gather x1, blocking collectives: 9.91 us -> 7.5 us  [on_device(): whole = lax.all_gather(fields[0], 'chan', axis=0, tiled=True)]
    unnamed x67 -> x112, local copies, waits for them, and re-layouts: 8.01 us -> 6.38 us
    ppermute x0 -> x1, starting transfers between devices: none -> 1.56 us  [on_device(): lax.ppermute(pieces[0], 'chan', [(i, (i + shift) % chans) for i in range(...]
  transfers between devices with their start and end apart: 5 -> 6, of which waited for: 4 -> 5; matrix products, arithmetic and copies ran while one was open for 14% -> 14% of each run, Pallas kernels for 0% -> 0%
where the time goes in v4:
time: 150 us; the launch traced here: 149 us
  Pallas kernels  41.7 us (28%)
  starting transfers between devices  23 us (15%)
  local copies, waits for them, and re-layouts  21.4 us (14%)
  matrix products  19.8 us (13%)
  waiting for transfers between devices  19 us (13%)
  other arithmetic  12.8 us (9%)
  blocking collectives  7.5 us (5%)
  between operations  3.54 us (2%)
    pallas_call x1, Pallas kernels, sum_over_patches(): pl.pallas_call(kernel, out_shape=[jax.ShapeDtypeStruct(a_full.shape, jnp....  41.7 us
    all_to_all x4, starting transfers between devices, swap(): lax.all_to_all(sent, 'patch', split_axis=0, concat_axis=0, tiled=True)  19.9 us
    all_to_all x4, waiting for transfers between devices, swap(): lax.all_to_all(sent, 'patch', split_axis=0, concat_axis=0, tiled=True)  12.3 us
    conv_general_dilated x3, matrix products, conv(): lax.conv_general_dilated(values[None], weight, (1, 1), ((pad, pad), (pad,...  11 us
    all_gather x1, blocking collectives, on_device(): whole = lax.all_gather(fields[0], 'chan', axis=0, tiled=True)  7.5 us
    unnamed x112, local copies, waits for them, and re-layouts  6.38 us
    ppermute x1, waiting for transfers between devices, on_device(): lax.ppermute(pieces[0], 'chan', [(i, (i + shift) % chans) for i in range(...  3.55 us
    ppermute x1, waiting for transfers between devices, on_device(): lax.ppermute(rounded, 'chan', [(i, (i + shift) % chans) for i in range(ch...  3.17 us
  transfers between devices with their start and end apart: 6, of which 5 were waited for; matrix products, arithmetic and copies ran while one was open for 14% of the time, Pallas kernels for 0%

profile of v4, /device:TPU:0, one launch (start us, length us, event | category | flops | bytes accessed | tf_op | source)
XLA Modules:
  0.0 148.7 jit_solution(2875687540458289108)
XLA Ops:
  0.7 7.5 %all-gather = bf16[1,128,1024]{2,1,0:T(8,128)(2,1)S(1)} all-gather(bf16[1,64,1024]{2,1,0:T(8,128)(2,1)} %param.10), channel_id=2, replica_groups=mesh['patch'=16,'chan'=2] {'chan'}, dimensions={1}, use_global_device_ids=true | all-gather | bytes 393216 | tf_op jit(solution)/shard_map/all_gather | solution.py:228
  9.0 0.3 convolution_convert_fusion.4
  9.3 0.7 copy.134
  10.0 6.1 %all-to-all-start = ((bf16[16,32,128]{2,1,0:T(8,128)(2,1)}), bf16[16,32,128]{2,1,0:T(8,128)(2,1)S(1)}, u32[]{:S(2)}, u32[]{:S(2)}) async-start(bf16[16,32,128]{2,1,0:T(8,128)(2,1)} %copy.134), calls=%async_computation | async-start | bytes 262144 | tf_op jit(solution)/shard_map/all_to_all | solution.py:226
  16.2 0.6 gather_fusion
  16.9 0.7 broadcast_select_fusion.5
  18.3 0.7 broadcast_in_dim.178
  19.0 0.7 broadcast_in_dim.184
  19.7 0.7 broadcast_in_dim.189
  20.4 0.7 broadcast_in_dim.194
  21.3 2.8 %all-to-all-done = bf16[16,32,128]{2,1,0:T(8,128)(2,1)S(1)} async-done(((bf16[16,32,128]{2,1,0:T(8,128)(2,1)}), bf16[16,32,128]{2,1,0:T(8,128)(2,1)S(1)}, u32[]{:S(2)}, u32[]{:S(2)}) %all-to-all-start) | async-done | bytes 131104 | tf_op jit(solution)/shard_map/all_to_all | solution.py:226
  24.7 3.6 %fusion.47 = f32[1,32,32,256]{3,0,2,1:T(1,128)S(1)} fusion(bf16[3,3,256,128]{3,2,1,0:T(8,128)(2,1)S(1)} %bitcast.347, bf16[1,34,34,128]{3,2,1,0:T(8,128)(2,1)S(1)} %maximum_bitcast_fusion.1), kind=kOutput, calls=%fused_computation.93 | convolution fusion | flops 603979776 | bytes 1934336 | tf_op jit(solution)/shard_map/conv_general_dilated | solution.py:25
  28.3 0.4 fusion.40
  29.0 0.3 copy-done.25
  29.5 0.8 broadcast_select_fusion.2
  30.4 0.9 convolution_convert_fusion.1
  31.3 0.8 copy.143
  32.1 0.8 copy.135
  32.8 4.2 %all-to-all-start.1 = ((bf16[16,65,64]{1,2,0:T(8,128)(2,1)}), bf16[16,65,64]{1,2,0:T(8,128)(2,1)}, u32[]{:S(2)}, u32[]{:S(2)}) async-start(bf16[16,65,64]{1,2,0:T(8,128)(2,1)} %copy.135), calls=%async_computation.1 | async-start | bytes 524288 | tf_op jit(solution)/shard_map/all_to_all | solution.py:226
  37.1 1.0 fusion.92
  38.1 1.0 fusion.91
  39.1 8.0 %all-to-all-done.1 = bf16[16,65,64]{1,2,0:T(8,128)(2,1)} async-done(((bf16[16,65,64]{1,2,0:T(8,128)(2,1)}), bf16[16,65,64]{1,2,0:T(8,128)(2,1)}, u32[]{:S(2)}, u32[]{:S(2)}) %all-to-all-start.1) | async-done | bytes 133152 | tf_op jit(solution)/shard_map/all_to_all | solution.py:226
  47.1 3.7 %all-to-all-start.2 = ((bf16[16,32,256]{2,1,0:T(8,128)(2,1)}), bf16[16,32,256]{2,1,0:T(8,128)(2,1)S(1)}, u32[]{:S(2)}, u32[]{:S(2)}) async-start(bf16[16,32,256]{2,1,0:T(8,128)(2,1)} %copy.143), calls=%async_computation.2 | async-start | bytes 524288 | tf_op jit(solution)/shard_map/all_to_all | solution.py:226
  50.8 1.1 copy.149
  51.9 1.6 %collective-permute-start.1 = (bf16[1024,64]{1,0:T(8,128)(2,1)S(1)}, bf16[1024,64]{1,0:T(8,128)(2,1)S(1)}, u32[]{:S(2)}, u32[]{:S(2)}) collective-permute-start(bf16[1024,64]{1,0:T(8,128)(2,1)S(1)} %bitcast.328), channel_id=1, source_target_pairs={{0,1},{1,0},{2,3},{3,2},{4,5},{5,4},{6,7},{7,6},{8,9},{9,8},{10,11... | collective-permute-start | bytes 393224 | tf_op jit(solution)/shard_map/ppermute | solution.py:249
  53.5 0.9 pad_maximum_fusion.4
  54.4 1.0 copy.168
  55.4 1.3 convert_reduce_fusion
  56.8 3.6 %collective-permute-done.1 = bf16[1024,64]{1,0:T(8,128)(2,1)S(1)} collective-permute-done((bf16[1024,64]{1,0:T(8,128)(2,1)S(1)}, bf16[1024,64]{1,0:T(8,128)(2,1)S(1)}, u32[]{:S(2)}, u32[]{:S(2)}) %collective-permute-start.1) | collective-permute-done | bytes 131104 | tf_op jit(solution)/shard_map/ppermute | solution.py:249
  60.3 0.8 broadcast_select_fusion.1
  61.6 1.0 pad_maximum_fusion.1
  62.6 0.4 maximum_bitcast_fusion
  63.1 0.5 pad_maximum_fusion
  63.5 3.9 %fusion = f32[1,32,32,128]{3,0,2,1:T(1,128)S(1)} fusion(bf16[3,3,128,256]{3,2,1,0:T(8,128)(2,1)S(1)} %bitcast.293, bf16[1,34,34,256]{3,2,1,0:T(8,128)(2,1)S(1)} %maximum_bitcast_fusion), kind=kOutput, calls=%fused_computation.9 | convolution fusion | flops 603979776 | bytes 1705984 | tf_op jit(solution)/shard_map/conv_general_dilated | solution.py:25
  67.5 1.6 %collective-permute-start = (bf16[1024,128]{1,0:T(8,128)(2,1)S(1)}, bf16[1024,128]{1,0:T(8,128)(2,1)S(1)}, u32[]{:S(2)}, u32[]{:S(2)}) collective-permute-start(bf16[1024,128]{1,0:T(8,128)(2,1)S(1)} %convert_element_type.98), channel_id=1, source_target_pairs={{0,1},{1,0},{2,3},{3,2},{4,5},{5,4},{6,7},{7,6},{8,9},{9,8},{10,11... | collective-permute-start | bytes 786440 | tf_op jit(solution)/shard_map/ppermute | solution.py:267
  69.0 1.3 fusion.88
  70.4 1.5 %fusion.87 = (bf16[32,32,256]{2,1,0:T(8,128)(2,1)}, bf16[32,32,256]{2,1,0:T(8,128)(2,1)}, bf16[32,32,256]{2,1,0:T(8,128)(2,1)}) fusion(bf16[34,33,256]{2,1,0:T(8,128)(2,1)S(1)} %get-tuple-element.26), kind=kLoop, calls=%fused_computation.181 | loop fusion | bytes 3145728 | tf_op jit(solution)/shard_map/slice | solution.py:279
  71.9 3.2 %collective-permute-done = bf16[1024,128]{1,0:T(8,128)(2,1)S(1)} collective-permute-done((bf16[1024,128]{1,0:T(8,128)(2,1)S(1)}, bf16[1024,128]{1,0:T(8,128)(2,1)S(1)}, u32[]{:S(2)}, u32[]{:S(2)}) %collective-permute-start) | collective-permute-done | bytes 262176 | tf_op jit(solution)/shard_map/ppermute | solution.py:267
  75.1 1.0 fusion.50
  76.2 0.3 convolution_convert_fusion.3
  76.6 0.7 copy.156
  77.2 5.9 %all-to-all-start.3 = ((bf16[16,32,128]{2,1,0:T(8,128)(2,1)}), bf16[16,32,128]{2,1,0:T(8,128)(2,1)S(1)}, u32[]{:S(2)}, u32[]{:S(2)}) async-start(bf16[16,32,128]{2,1,0:T(8,128)(2,1)} %copy.156), calls=%async_computation.3 | async-start | bytes 262144 | tf_op jit(solution)/shard_map/all_to_all | solution.py:226
  83.1 3.5 %fusion.51 = f32[1,32,32,256]{3,0,2,1:T(1,128)S(1)} fusion(bf16[3,3,128,256]{3,2,1,0:T(8,128)(2,1)S(1)} %bitcast.294, bf16[1,32,32,128]{3,2,1,0:T(8,128)(2,1)S(1)} %bitcast.309), kind=kOutput, calls=%fused_computation.101 | convolution fusion | flops 579076096 | bytes 1900544 | tf_op jit(solution)/shard_map/conv_general_dilated | solution.py:25
  86.7 1.1 copy.172
  89.5 1.5 %all-to-all-done.3 = bf16[16,32,128]{2,1,0:T(8,128)(2,1)S(1)} async-done(((bf16[16,32,128]{2,1,0:T(8,128)(2,1)}), bf16[16,32,128]{2,1,0:T(8,128)(2,1)S(1)}, u32[]{:S(2)}, u32[]{:S(2)}) %all-to-all-start.3) | async-done | bytes 131104 | tf_op jit(solution)/shard_map/all_to_all | solution.py:226
  91.4 0.4 convolution_convert_fusion
  92.3 1.6 %fusion.85 = (f32[256]{0:T(256)S(1)}, bf16[1,32,32,256]{3,2,1,0:T(8,128)(2,1)S(1)}) fusion(f32[256]{0:T(256)S(1)} %copy-done.36, f32[1,32,32,256]{3,0,2,1:T(1,128)S(1)} %fusion.47, f32[32,256]{1,0:T(8,128)S(1)} %get-tuple-element.55, pred[32]{0:T(512)(128)(4,1)S(1)} %copy-done.38, f32[32,256]{1,0:T(8,128)S(1)} %get-tuple-element.56, ...), kind=kLoop, calls=%fused_computation.180 | loop fusion | flops 7864064 | bytes 2754624 | tf_op jit(solution)/shard_map/reduce_sum | solution.py:319
  93.9 0.3 fusion.10
  94.3 0.3 fusion.9
  94.8 0.3 fusion.8
  95.2 0.3 fusion.7
  95.5 0.3 copy-done.2
  95.9 1.9 %fusion.26 = (bf16[1024,256]{1,0:T(8,128)(2,1)S(1)}, bf16[1024,256]{1,0:T(8,128)(2,1)S(1)}) fusion(f32[1,32,32,256]{3,2,0,1:T(8,128)S(1)} %copy-done.2, f32[1,32,32,256]{3,2,0,1:T(8,128)S(1)} %copy-done.1, f32[32,256]{1,0:T(8,128)S(1)} %get-tuple-element.55, f32[32,256]{1,0:T(8,128)S(1)} %get-tuple-element.56, f32[32,256]{1,0:T(8,128)S(1)} %get-tuple-element.57, ...), kind=kLoop, calls=%fused_computation.57 | loop fusion | flops 8126464 | bytes 3281920 | tf_op jit(solution)/shard_map/convert_element_type | solution.py:320
  97.8 0.3 fusion.6
  98.2 0.3 fusion.5
  98.7 0.3 fusion.4
  99.1 0.3 fusion.3
  99.4 0.3 fusion.2
  99.8 0.6 fusion.72.refs_2_
  102.1 41.7 %shard_map.129 = (f32[1152,256]{1,0:T(8,128)S(1)}, f32[2304,128]{1,0:T(8,128)S(1)}, f32[8,128]{1,0:T(8,128)S(1)}) custom-call(f32[1152,256]{1,0:T(8,128)S(1)} %bitcast.296, f32[2304,128]{1,0:T(8,128)S(1)} %bitcast.297, f32[8,128]{1,0:T(8,128)S(1)} %fusion.72.refs_2_), custom_call_target="tpu_custom_call" | custom-call | tf_op jit(solution)/shard_map/pallas_call | solution.py:176
  143.8 0.5 slice.224
  144.4 0.6 slice_bitcast_fusion.8
  145.6 1.0 copy.251
  146.6 1.0 copy.252
  (171 shorter events, 8.0 us)
Async XLA Ops:
  0.6 62.9 %copy-start = (bf16[9,128,256]{2,1,0:T(8,128)(2,1)S(1)}, bf16[9,128,256]{2,1,0:T(8,128)(2,1)}, u32[]{:S(2)}) copy-start(bf16[9,128,256]{2,1,0:T(8,128)(2,1)} %param.13) | copy-start | bytes 1769476
  0.6 15.6 %copy-start.30 = (s32[4,3]{1,0:T(4,128)S(1)}, s32[4,3]{1,0:T(4,128)}, u32[]{:S(2)}) copy-start(s32[4,3]{1,0:T(4,128)} %constant.75.clone) | copy-start | bytes 148
  0.7 7.8 %copy-start.42 = (s32[16,4]{0,1:T(4,128)S(1)}, s32[16,4]{0,1:T(4,128)}, u32[]{:S(2)}) copy-start(s32[16,4]{0,1:T(4,128)} %param.15) | copy-start | bytes 772
  0.7 8.0 %copy-start.48 = (s32[16,4]{0,1:T(4,128)S(1)}, s32[16,4]{0,1:T(4,128)}, u32[]{:S(2)}) copy-start(s32[16,4]{0,1:T(4,128)} %param.14) | copy-start | bytes 772
  0.7 16.9 %copy-start.47 = (bf16[1,1024]{1,0:T(2,128)(2,1)S(1)}, bf16[1,1024]{1,0:T(2,128)(2,1)}, u32[]{:S(2)}) copy-start(bf16[1,1024]{1,0:T(2,128)(2,1)} %param.18) | copy-start | bytes 6148
  0.7 17.3 %copy-start.29 = (bf16[1,64,1024]{2,1,0:T(8,128)(2,1)S(1)}, bf16[1,64,1024]{2,1,0:T(8,128)(2,1)}, u32[]{:S(2)}) copy-start(bf16[1,64,1024]{2,1,0:T(8,128)(2,1)} %param.17) | copy-start | bytes 393220
  8.2 10.0 %copy-start.5 = (bf16[1,128,1024]{2,1,0:T(8,128)(2,1)}, bf16[1,128,1024]{2,1,0:T(8,128)(2,1)S(1)}, u32[]{:S(2)}) copy-start(bf16[1,128,1024]{2,1,0:T(8,128)(2,1)S(1)} %all-gather) | copy-start | bytes 786436
  8.2 12.8 %copy-start.49 = (s32[16]{0:T(128)S(1)}, s32[16]{0:T(128)}, u32[]{:S(2)}) copy-start(s32[16]{0:T(128)} %param.16) | copy-start | bytes 196
  8.7 8.9 %copy-start.33 = (pred[4]{0:T(512)(128)(4,1)}, pred[4]{0:T(512)(128)(4,1)S(1)}, u32[]{:S(2)}) copy-start(pred[4]{0:T(512)(128)(4,1)S(1)} %compare_reduce_fusion) | copy-start | bytes 16
  8.9 15.2 %copy-start.31 = (s32[4]{0:T(128)}, s32[4]{0:T(128)S(1)}, u32[]{:S(2)}) copy-start(s32[4]{0:T(128)S(1)} %get-tuple-element.70) | copy-start | bytes 52
  10.0 14.1 %all-to-all-start = ((bf16[16,32,128]{2,1,0:T(8,128)(2,1)}), bf16[16,32,128]{2,1,0:T(8,128)(2,1)S(1)}, u32[]{:S(2)}, u32[]{:S(2)}) async-start(bf16[16,32,128]{2,1,0:T(8,128)(2,1)} %copy.134), calls=%async_computation | async-start | bytes 262144 | tf_op jit(solution)/shard_map/all_to_all | solution.py:226
  17.5 7.0 %copy-start.37 = (pred[32]{0:T(512)(128)(4,1)}, pred[32]{0:T(512)(128)(4,1)S(1)}, u32[]{:S(2)}) copy-start(pred[32]{0:T(512)(128)(4,1)S(1)} %get-tuple-element.72) | copy-start | bytes 100
  17.5 7.0 %copy-start.39 = (pred[32]{0:T(512)(128)(4,1)}, pred[32]{0:T(512)(128)(4,1)S(1)}, u32[]{:S(2)}) copy-start(pred[32]{0:T(512)(128)(4,1)S(1)} %get-tuple-element.73) | copy-start | bytes 100
  18.0 6.7 %copy-start.50 = (bf16[9,256,128]{2,1,0:T(8,128)(2,1)S(1)}, bf16[9,256,128]{2,1,0:T(8,128)(2,1)}, u32[]{:S(2)}) copy-start(bf16[9,256,128]{2,1,0:T(8,128)(2,1)} %param.11) | copy-start | bytes 1769476
  24.4 4.4 %copy-start.27 = (bf16[1,32,128]{2,1,0:T(8,128)(2,1)}, bf16[1,32,128]{2,1,0:T(8,128)(2,1)S(1)}, u32[]{:S(2)}) copy-start(bf16[1,32,128]{2,1,0:T(8,128)(2,1)S(1)} %copy.138) | copy-start | bytes 24580
  24.7 3.6 %copy-start.35 = (f32[256]{0:T(256)S(1)}, f32[256]{0:T(256)}, u32[]{:S(2)}) copy-start(f32[256]{0:T(256)} %param.12) | copy-start | bytes 3076
  28.8 0.6 copy-start.25
  28.8 0.6 copy-start.26
  32.8 14.3 %all-to-all-start.1 = ((bf16[16,65,64]{1,2,0:T(8,128)(2,1)}), bf16[16,65,64]{1,2,0:T(8,128)(2,1)}, u32[]{:S(2)}, u32[]{:S(2)}) async-start(bf16[16,65,64]{1,2,0:T(8,128)(2,1)} %copy.135), calls=%async_computation.1 | async-start | bytes 524288 | tf_op jit(solution)/shard_map/all_to_all | solution.py:226
  38.1 15.4 %copy-start.28 = (bf16[1,32,128]{2,1,0:T(8,128)(2,1)S(1)}, bf16[1,32,128]{2,1,0:T(8,128)(2,1)}, u32[]{:S(2)}) copy-start(bf16[1,32,128]{2,1,0:T(8,128)(2,1)} %copy-done.27) | copy-start | bytes 24580
  47.1 14.1 %all-to-all-start.2 = ((bf16[16,32,256]{2,1,0:T(8,128)(2,1)}), bf16[16,32,256]{2,1,0:T(8,128)(2,1)S(1)}, u32[]{:S(2)}, u32[]{:S(2)}) async-start(bf16[16,32,256]{2,1,0:T(8,128)(2,1)} %copy.143), calls=%async_computation.2 | async-start | bytes 524288 | tf_op jit(solution)/shard_map/all_to_all | solution.py:226
  51.9 8.4 %collective-permute-start.1 = (bf16[1024,64]{1,0:T(8,128)(2,1)S(1)}, bf16[1024,64]{1,0:T(8,128)(2,1)S(1)}, u32[]{:S(2)}, u32[]{:S(2)}) collective-permute-start(bf16[1024,64]{1,0:T(8,128)(2,1)S(1)} %bitcast.328), channel_id=1, source_target_pairs={{0,1},{1,0},{2,3},{3,2},{4,5},{5,4},{6,7},{7,6},{8,9},{9,8},{10,11... | collective-permute-start | bytes 393224 | tf_op jit(solution)/shard_map/ppermute | solution.py:249
  55.4 5.8 %copy-start.32 = (s32[4]{0:T(128)S(1)}, s32[4]{0:T(128)}, u32[]{:S(2)}) copy-start(s32[4]{0:T(128)} %copy-done.31) | copy-start | bytes 52
  67.5 7.6 %collective-permute-start = (bf16[1024,128]{1,0:T(8,128)(2,1)S(1)}, bf16[1024,128]{1,0:T(8,128)(2,1)S(1)}, u32[]{:S(2)}, u32[]{:S(2)}) collective-permute-start(bf16[1024,128]{1,0:T(8,128)(2,1)S(1)} %convert_element_type.98), channel_id=1, source_target_pairs={{0,1},{1,0},{2,3},{3,2},{4,5},{5,4},{6,7},{7,6},{8,9},{9,8},{10,11... | collective-permute-start | bytes 786440 | tf_op jit(solution)/shard_map/ppermute | solution.py:267
  70.4 4.7 %copy-start.23 = (bf16[1024,64]{1,0:T(8,128)(2,1)S(1)}, bf16[1024,64]{1,0:T(8,128)(2,1)}, u32[]{:S(2)}) copy-start(bf16[1024,64]{1,0:T(8,128)(2,1)} %get-tuple-element.34) | copy-start | bytes 393220
  70.4 4.7 %copy-start.24 = (bf16[1024,64]{1,0:T(8,128)(2,1)S(1)}, bf16[1024,64]{1,0:T(8,128)(2,1)}, u32[]{:S(2)}) copy-start(bf16[1024,64]{1,0:T(8,128)(2,1)} %get-tuple-element.35) | copy-start | bytes 393220
  71.9 4.3 %copy-start.34 = (pred[4]{0:T(512)(128)(4,1)S(1)}, pred[4]{0:T(512)(128)(4,1)}, u32[]{:S(2)}) copy-start(pred[4]{0:T(512)(128)(4,1)} %copy-done.33) | copy-start | bytes 16
  77.2 13.8 %all-to-all-start.3 = ((bf16[16,32,128]{2,1,0:T(8,128)(2,1)}), bf16[16,32,128]{2,1,0:T(8,128)(2,1)S(1)}, u32[]{:S(2)}, u32[]{:S(2)}) async-start(bf16[16,32,128]{2,1,0:T(8,128)(2,1)} %copy.156), calls=%async_computation.3 | async-start | bytes 262144 | tf_op jit(solution)/shard_map/all_to_all | solution.py:226
  86.7 1.4 copy-start.3
  86.7 1.4 copy-start.13
  86.7 1.9 %copy-start.8 = (bf16[32,32,256]{2,1,0:T(8,128)(2,1)S(1)}, bf16[32,32,256]{2,1,0:T(8,128)(2,1)}, u32[]{:S(2)}) copy-start(bf16[32,32,256]{2,1,0:T(8,128)(2,1)} %get-tuple-element.29) | copy-start | bytes 1572868
  87.8 1.1 copy-start.14
  88.1 1.1 copy-start.12
  88.9 2.5 %copy-start.41 = (s32[4,3]{1,0:T(4,128)S(1)}, s32[4,3]{1,0:T(4,128)}, u32[]{:S(2)}) copy-start(s32[4,3]{1,0:T(4,128)} %broadcast_select_fusion.5) | copy-start | bytes 148
  89.5 2.6 %copy-start.36 = (f32[256]{0:T(256)S(1)}, f32[256]{0:T(256)}, u32[]{:S(2)}) copy-start(f32[256]{0:T(256)} %param.12) | copy-start | bytes 3076
  89.5 2.6 %copy-start.38 = (pred[32]{0:T(512)(128)(4,1)S(1)}, pred[32]{0:T(512)(128)(4,1)}, u32[]{:S(2)}) copy-start(pred[32]{0:T(512)(128)(4,1)} %copy-done.37) | copy-start | bytes 100
  89.5 2.6 %copy-start.40 = (pred[32]{0:T(512)(128)(4,1)S(1)}, pred[32]{0:T(512)(128)(4,1)}, u32[]{:S(2)}) copy-start(pred[32]{0:T(512)(128)(4,1)} %copy-done.39) | copy-start | bytes 100
  91.0 1.2 copy-start.4
  92.3 1.6 %copy-start.21 = (bf16[32,32,128]{2,1,0:T(8,128)(2,1)S(1)}, bf16[32,32,128]{2,1,0:T(8,128)(2,1)}, u32[]{:S(2)}) copy-start(bf16[32,32,128]{2,1,0:T(8,128)(2,1)} %get-tuple-element.41) | copy-start | bytes 786436
  92.3 2.0 %copy-start.16 = (bf16[32,32,128]{2,1,0:T(8,128)(2,1)S(1)}, bf16[32,32,128]{2,1,0:T(8,128)(2,1)}, u32[]{:S(2)}) copy-start(bf16[32,32,128]{2,1,0:T(8,128)(2,1)} %get-tuple-element.45) | copy-start | bytes 786436
  93.9 1.0 copy-start.22
  93.9 1.3 copy-start.20
  94.3 1.3 copy-start.1
  94.3 1.6 %copy-start.2 = (f32[1,32,32,256]{3,2,0,1:T(8,128)S(1)}, f32[1,32,32,256]{3,2,0,1:T(8,128)}, u32[]{:S(2)}) copy-start(f32[1,32,32,256]{3,2,0,1:T(8,128)} %copy.172) | copy-start | bytes 3145732
  94.3 1.6 %copy-start.43 = (pred[1024]{0:T(1024)(128)(4,1)S(1)}, pred[1024]{0:T(1024)(128)(4,1)}, u32[]{:S(2)}) copy-start(pred[1024]{0:T(1024)(128)(4,1)} %broadcast_in_dim.178) | copy-start | bytes 3076
  94.3 1.6 %copy-start.44 = (pred[1024]{0:T(1024)(128)(4,1)S(1)}, pred[1024]{0:T(1024)(128)(4,1)}, u32[]{:S(2)}) copy-start(pred[1024]{0:T(1024)(128)(4,1)} %broadcast_in_dim.184) | copy-start | bytes 3076
  94.3 1.5 %copy-start.45 = (pred[1024]{0:T(1024)(128)(4,1)S(1)}, pred[1024]{0:T(1024)(128)(4,1)}, u32[]{:S(2)}) copy-start(pred[1024]{0:T(1024)(128)(4,1)} %broadcast_in_dim.189) | copy-start | bytes 3076
  94.3 1.5 %copy-start.46 = (pred[1024]{0:T(1024)(128)(4,1)S(1)}, pred[1024]{0:T(1024)(128)(4,1)}, u32[]{:S(2)}) copy-start(pred[1024]{0:T(1024)(128)(4,1)} %broadcast_in_dim.194) | copy-start | bytes 3076
  95.8 1.9 %copy-start.6 = (bf16[1,128,1024]{2,1,0:T(8,128)(2,1)S(1)}, bf16[1,128,1024]{2,1,0:T(8,128)(2,1)}, u32[]{:S(2)}) copy-start(bf16[1,128,1024]{2,1,0:T(8,128)(2,1)} %copy-done.5) | copy-start | bytes 786436
  95.9 2.3 %copy-start.19 = (bf16[32,32,128]{2,1,0:T(8,128)(2,1)S(1)}, bf16[32,32,128]{2,1,0:T(8,128)(2,1)}, u32[]{:S(2)}) copy-start(bf16[32,32,128]{2,1,0:T(8,128)(2,1)} %get-tuple-element.37) | copy-start | bytes 786436
  97.8 1.0 copy-start.18
  97.8 1.3 copy-start.15
  98.2 1.3 copy-start.17
  99.1 1.7 %copy-start.11 = (bf16[32,32,256]{2,1,0:T(8,128)(2,1)S(1)}, bf16[32,32,256]{2,1,0:T(8,128)(2,1)}, u32[]{:S(2)}) copy-start(bf16[32,32,256]{2,1,0:T(8,128)(2,1)} %get-tuple-element.21) | copy-start | bytes 1572868
  99.4 1.6 %copy-start.10 = (bf16[32,32,256]{2,1,0:T(8,128)(2,1)S(1)}, bf16[32,32,256]{2,1,0:T(8,128)(2,1)}, u32[]{:S(2)}) copy-start(bf16[32,32,256]{2,1,0:T(8,128)(2,1)} %get-tuple-element.23) | copy-start | bytes 1572868
  100.4 1.1 copy-start.7
  100.7 1.1 copy-start.9

commit v5 on v3

--- a/solution.py
+++ b/solution.py
@@ -44,7 +44,9 @@
     return place + bit - 2 * bit * (lax.div(place, bit) % 2)
 
 
-def sum_kernel(count, chans, a_in, b_in, s_in, a_out, b_out, s_out, a_rec, b_rec, s_rec, send, recv):
+def sum_kernel(
+    count, chans, a_in, pre, taps, s_in, a_out, b_out, s_out, b_in, a_rec, b_rec, s_rec, send, recv
+):
     place = lax.axis_index("patch")
     lane = lax.axis_index("chan")
     bits = bits_of(count)
@@ -121,7 +123,29 @@
         one["start"] = one["start"] - mine * rows
         one["rows"] = 2 * rows
 
-    for one in streams:
+    inner = pre.shape[1]
+
+    def products(low, high):
+        for tap in range(low, high):
+            rows = taps[tap % 3, tap // 3 : tap // 3 + P_SIZE]
+            b_in[pl.ds(tap * inner, inner)] = lax.dot_general(
+                pre[...],
+                rows.reshape(P_SIZE * P_SIZE, rows.shape[-1]),
+                (((0,), (0,)), ((), ())),
+                preferred_element_type=jnp.float32,
+            )
+
+    for one in groups[0]:
+        scatter(one, 0)
+    done = 0
+    if b_in.shape[0] > 9 * inner:
+        b_in[pl.ds(9 * inner, b_in.shape[0] - 9 * inner)] = jnp.zeros(
+            (b_in.shape[0] - 9 * inner, b_in.shape[1]), jnp.float32
+        )
+    for one in groups[1]:
+        due = min(9, -(-(one["at"] + one["rows"]) // inner))
+        products(done, due)
+        done = due
         scatter(one, 0)
     small = send_to(s_out, s_rec.at[0], target(bits[0]))
     for stage in range(stages):
@@ -154,7 +178,7 @@
                 gather(one, stage - 1)
 
 
-def sum_over_patches(a, b, small):
+def sum_over_patches(a, pre, taps, small):
     count = lax.axis_size("patch")
     chans = lax.axis_size("chan")
     stages = len(bits_of(count))
@@ -164,9 +188,9 @@
     def padded(rows):
         return -(-rows // unit) * unit
 
-    a_rows, b_rows = padded(a.shape[0]), padded(b.shape[0])
+    a_rows, b_rows = padded(a.shape[0]), padded(9 * pre.shape[1])
     a_full = jnp.pad(a, ((0, a_rows - a.shape[0]), (0, 0)))
-    b_full = jnp.pad(b, ((0, b_rows - b.shape[0]), (0, 0)))
+    b_shape = (b_rows, taps.shape[-1])
     copies = 9 * stages + chan_stages
     spec = pl.BlockSpec(memory_space=pltpu.VMEM)
 
@@ -177,14 +201,15 @@
         kernel,
         out_shape=[
             jax.ShapeDtypeStruct(a_full.shape, jnp.float32),
-            jax.ShapeDtypeStruct(b_full.shape, jnp.float32),
+            jax.ShapeDtypeStruct(b_shape, jnp.float32),
             jax.ShapeDtypeStruct(small.shape, jnp.float32),
         ],
-        in_specs=[spec] * 3,
+        in_specs=[spec] * 4,
         out_specs=[spec] * 3,
         scratch_shapes=[
+            pltpu.VMEM(b_shape, jnp.float32),
             pltpu.VMEM((a_rows, a.shape[1]), jnp.float32),
-            pltpu.VMEM((b_rows, b.shape[1]), jnp.float32),
+            pltpu.VMEM(b_shape, jnp.float32),
             pltpu.VMEM((stages + chan_stages,) + small.shape, jnp.float32),
             pltpu.SemaphoreType.DMA((copies,)),
             pltpu.SemaphoreType.DMA((copies,)),
@@ -192,8 +217,8 @@
         compiler_params=pltpu.CompilerParams(
             collective_id=0, has_side_effects=True, vmem_limit_bytes=24 << 20
         ),
-    )(a_full, b_full, small)
-    return a_sum[: a.shape[0]], b_sum[: b.shape[0]], s_sum
+    )(a_full, pre, taps, small)
+    return a_sum[: a.shape[0]], b_sum[: 9 * pre.shape[1]], s_sum
 
 
 def on_device(fields, w_one, bias_one, w_two, neighbour, seam_code, band_order, target, lat_weight):
@@ -225,16 +250,25 @@
     def swap(sent):
         return lax.all_to_all(sent, "patch", split_axis=0, concat_axis=0, tiled=True)
 
-    both = lax.all_gather(jnp.stack([fields[0], target[0]]), "chan", axis=1, tiled=True)
-    chan_full = both.shape[1]
-    x_grid = both[0].T.reshape(length, length, chan_full)
+    lane = lax.axis_index("chan")
+    pieces = [target[0]]
+    for shift in range(1, chans):
+        pieces.append(
+            lax.ppermute(target[0], "chan", [(i, (i + shift) % chans) for i in range(chans)])
+        )
+    target_full = jnp.concatenate(
+        [lax.select_n((lane - c + chans) % chans, *pieces) for c in range(chans)], axis=0
+    )
+    whole = lax.all_gather(fields[0], "chan", axis=0, tiled=True)
+    chan_full = whole.shape[0]
+    x_grid = whole.T.reshape(length, length, chan_full)
     slots = (band_order[None, :] == ids[:, None]).astype(jnp.bfloat16)
     lat_rows = -(-part // chan_full)
     lat_parts = jnp.pad(
         lat_weight.reshape(count, part), ((0, 0), (0, lat_rows * chan_full - part))
     ).reshape(count, lat_rows, chan_full)
     band_parts = jnp.concatenate(
-        [both[1].T.reshape(count, part, chan_full), lat_parts], axis=1
+        [target_full.T.reshape(count, part, chan_full), lat_parts], axis=1
     )
     band_parts = jnp.einsum(
         "ps,skc->pkc", slots, band_parts, preferred_element_type=jnp.float32
@@ -311,19 +345,7 @@
     grad_pre = jax.vjp(smooth_gate, preact)[1](grad_h)[0].reshape(cells, inner)
     bias_local = jnp.sum(grad_pre, axis=0)
     pre_b = grad_pre.astype(jnp.bfloat16)
-    x_taps = [
-        x_pad[a : a + length, b : b + length].reshape(cells, chan_full)
-        for a in range(3)
-        for b in range(3)
-    ]
-    one_local = jnp.stack(
-        [
-            lax.dot_general(
-                pre_b, tap, (((0,), (0,)), ((), ())), preferred_element_type=jnp.float32
-            )
-            for tap in x_taps
-        ]
-    )
+    x_taps = jnp.stack([x_pad[:, b : b + length] for b in range(3)])
     small_rows = -(-(inner // chan_full + 1) // 8) * 8
     small = jnp.concatenate(
         [
@@ -332,7 +354,7 @@
         ]
     ).reshape(small_rows, chan_full)
     sum_two, sum_one, sum_small = sum_over_patches(
-        two_local.reshape(9 * chan_full, inner), one_local.reshape(9 * inner, chan_full), small
+        two_local.reshape(9 * chan_full, inner), pre_b, x_taps, small
     )
     grad_one = sum_one.reshape(9, inner, chan_full)
     grad_two = sum_two.reshape(9, chan_full, inner)

time: 144 us -> 141 us (0.979)
  matrix products: 21.2 us -> 17.1 us
  starting transfers between devices: 20.8 us -> 23.8 us
  local copies, waits for them, and re-layouts: 19.2 us -> 16.9 us
  waiting for transfers between devices: 15.9 us -> 17.8 us
    dot_general x9 -> x0, matrix products: 3.03 us -> none  [on_device(): lax.dot_general(pre_b, tap, (((0,), (0,)), ((), ())), preferred_element_t...]
    ppermute x0 -> x1, starting transfers between devices: none -> 3 us  [on_device(): lax.ppermute(target[0], 'chan', [(i, (i + shift) % chans) for i in range(...]
    slice x6 -> x0, local copies, waits for them, and re-layouts: 2.78 us -> none  [the longest x2 1.99 us: on_device(): x_pad[a:a + length, b:b + length].reshape(cells, chan_full)]
    convert_element_type x0 -> x1, other arithmetic: none -> 1.89 us  [on_device(): pre_b = grad_pre.astype(jnp.bfloat16)]
    all_to_all x4, waiting for transfers between devices: 12.9 us -> 14.4 us  [swap(): lax.all_to_all(sent, 'patch', split_axis=0, concat_axis=0, tiled=True)]
    unnamed x67 -> x55, local copies, waits for them, and re-layouts: 8.01 us -> 7.15 us
  transfers between devices with their start and end apart: 5 -> 6, of which waited for: 4 -> 4; matrix products, arithmetic and copies ran while one was open for 14% -> 16% of each run, Pallas kernels for 0% -> 0%
where the time goes in v5:
time: 141 us; the launch traced here: 140 us
  Pallas kernels  42.1 us (30%)
  starting transfers between devices  23.8 us (17%)
  waiting for transfers between devices  17.8 us (13%)
  matrix products  17.1 us (12%)
  local copies, waits for them, and re-layouts  16.9 us (12%)
  other arithmetic  10.3 us (7%)
  blocking collectives  9.12 us (6%)
  between operations  3.2 us (2%)
    pallas_call x1, Pallas kernels, sum_over_patches(): pl.pallas_call(kernel, out_shape=[jax.ShapeDtypeStruct(a_full.shape, jnp....  42.1 us
    all_to_all x4, starting transfers between devices, swap(): lax.all_to_all(sent, 'patch', split_axis=0, concat_axis=0, tiled=True)  19.3 us
    all_to_all x4, waiting for transfers between devices, swap(): lax.all_to_all(sent, 'patch', split_axis=0, concat_axis=0, tiled=True)  14.4 us
    conv_general_dilated x3, matrix products, conv(): lax.conv_general_dilated(values[None], weight, (1, 1), ((pad, pad), (pad,...  12.1 us
    all_gather x1, blocking collectives, on_device(): whole = lax.all_gather(fields[0], 'chan', axis=0, tiled=True)  9.12 us
    unnamed x55, local copies, waits for them, and re-layouts  7.15 us
    ppermute x1, waiting for transfers between devices, on_device(): lax.ppermute(rounded, 'chan', [(i, (i + shift) % chans) for i in range(ch...  3.39 us
    ppermute x1, starting transfers between devices, on_device(): lax.ppermute(target[0], 'chan', [(i, (i + shift) % chans) for i in range(...  3 us
  transfers between devices with their start and end apart: 6, of which 4 were waited for; matrix products, arithmetic and copies ran while one was open for 16% of the time, Pallas kernels for 0%

profile of v5, /device:TPU:0, one launch (start us, length us, event | category | flops | bytes accessed | tf_op | source)
XLA Modules:
  0.0 140.3 jit_solution(345458209653164323)
XLA Ops:
  0.7 1.1 copy.154
  1.8 3.0 %collective-permute-start = (bf16[64,1024]{0,1:T(8,128)(2,1)S(1)}, bf16[64,1024]{0,1:T(8,128)(2,1)S(1)}, u32[]{:S(2)}, u32[]{:S(2)}) collective-permute-start(bf16[64,1024]{0,1:T(8,128)(2,1)S(1)} %bitcast.260), channel_id=1, source_target_pairs={{0,1},{1,0},{2,3},{3,2},{4,5},{5,4},{6,7},{7,6},{8,9},{9,8},{10,11... | collective-permute-start | bytes 393224 | tf_op jit(solution)/shard_map/ppermute | solution.py:257
  4.8 9.1 %all-gather = bf16[1,128,1024]{2,1,0:T(8,128)(2,1)S(1)} all-gather(bf16[1,64,1024]{2,1,0:T(8,128)(2,1)} %param.10), channel_id=2, replica_groups=mesh['patch'=16,'chan'=2] {'chan'}, dimensions={1}, use_global_device_ids=true | all-gather | bytes 393216 | tf_op jit(solution)/shard_map/all_gather | solution.py:262
  14.2 0.2 compare_reduce_fusion
  14.4 0.2 dynamic-slice_reduce_fusion
  14.7 0.3 convolution_convert_fusion.4
  15.0 0.7 copy.158
  15.7 6.2 %all-to-all-start = ((bf16[16,32,128]{2,1,0:T(8,128)(2,1)}), bf16[16,32,128]{2,1,0:T(8,128)(2,1)S(1)}, u32[]{:S(2)}, u32[]{:S(2)}) async-start(bf16[16,32,128]{2,1,0:T(8,128)(2,1)} %copy.158), calls=%async_computation | async-start | bytes 262144 | tf_op jit(solution)/shard_map/all_to_all | solution.py:251
  22.5 0.2 copy-done.21
  22.8 0.2 convolution_convert_fusion.1
  23.0 6.9 %all-to-all-done = bf16[16,32,128]{2,1,0:T(8,128)(2,1)S(1)} async-done(((bf16[16,32,128]{2,1,0:T(8,128)(2,1)}), bf16[16,32,128]{2,1,0:T(8,128)(2,1)S(1)}, u32[]{:S(2)}, u32[]{:S(2)}) %all-to-all-start) | async-done | bytes 131104 | tf_op jit(solution)/shard_map/all_to_all | solution.py:251
  29.9 0.2 fusion.57
  30.4 4.6 %fusion.39 = f32[1,32,32,256]{3,0,2,1:T(1,128)S(1)} fusion(bf16[3,3,256,128]{3,2,1,0:T(8,128)(2,1)} %bitcast.272, bf16[1,34,34,128]{3,2,1,0:T(8,128)(2,1)S(1)} %maximum_bitcast_fusion.1), kind=kOutput, calls=%fused_computation.76 | convolution fusion | flops 603979776 | bytes 1934336 | tf_op jit(solution)/shard_map/conv_general_dilated | solution.py:25
  35.0 0.4 fusion.32
  35.7 0.4 convolution_convert_fusion.2
  36.0 0.8 copy.167
  36.8 3.5 %all-to-all-start.2 = ((bf16[16,32,256]{2,1,0:T(8,128)(2,1)}), bf16[16,32,256]{2,1,0:T(8,128)(2,1)S(1)}, u32[]{:S(2)}, u32[]{:S(2)}) async-start(bf16[16,32,256]{2,1,0:T(8,128)(2,1)} %copy.167), calls=%async_computation.2 | async-start | bytes 524288 | tf_op jit(solution)/shard_map/all_to_all | solution.py:251
  40.4 0.6 gather_fusion
  41.5 0.7 broadcast_in_dim.185
  42.2 1.0 copy.189
  43.2 0.8 copy.159
  44.0 0.3 fusion.49
  44.4 6.0 %all-to-all-done.2 = bf16[16,32,256]{2,1,0:T(8,128)(2,1)S(1)} async-done(((bf16[16,32,256]{2,1,0:T(8,128)(2,1)}), bf16[16,32,256]{2,1,0:T(8,128)(2,1)S(1)}, u32[]{:S(2)}, u32[]{:S(2)}) %all-to-all-start.2) | async-done | bytes 262176 | tf_op jit(solution)/shard_map/all_to_all | solution.py:251
  50.4 3.7 %all-to-all-start.1 = ((bf16[16,65,128]{2,1,0:T(8,128)(2,1)}), bf16[16,65,128]{2,1,0:T(8,128)(2,1)S(1)}, u32[]{:S(2)}, u32[]{:S(2)}) async-start(bf16[16,65,128]{2,1,0:T(8,128)(2,1)} %copy.159), calls=%async_computation.1 | async-start | bytes 589824 | tf_op jit(solution)/shard_map/all_to_all | solution.py:251
  54.1 0.3 fusion.53
  54.5 0.4 maximum_bitcast_fusion
  54.9 0.4 pad_maximum_fusion.1
  55.4 3.9 %fusion = f32[1,32,32,128]{3,0,2,1:T(1,128)S(1)} fusion(bf16[3,3,128,256]{3,2,1,0:T(8,128)(2,1)S(1)} %bitcast.237, bf16[1,34,34,256]{3,2,1,0:T(8,128)(2,1)S(1)} %maximum_bitcast_fusion), kind=kOutput, calls=%fused_computation.9 | convolution fusion | flops 603979776 | bytes 1705984 | tf_op jit(solution)/shard_map/conv_general_dilated | solution.py:25
  59.3 0.8 convert_element_type.91
  60.1 1.5 %collective-permute-start.1 = (bf16[1024,128]{1,0:T(8,128)(2,1)}, bf16[1024,128]{1,0:T(8,128)(2,1)}, u32[]{:S(2)}, u32[]{:S(2)}) collective-permute-start(bf16[1024,128]{1,0:T(8,128)(2,1)} %convert_element_type.91), channel_id=1, source_target_pairs={{0,1},{1,0},{2,3},{3,2},{4,5},{5,4},{6,7},{7,6},{8,9},{9,8},{10,11... | collective-permute-start | bytes 786440 | tf_op jit(solution)/shard_map/ppermute | solution.py:294
  61.6 1.2 fusion.80
  62.9 1.5 %fusion.79 = (bf16[32,32,256]{2,1,0:T(8,128)(2,1)}, bf16[32,32,256]{2,1,0:T(8,128)(2,1)}, bf16[32,32,256]{2,1,0:T(8,128)(2,1)}) fusion(bf16[34,33,256]{2,1,0:T(8,128)(2,1)S(1)} %get-tuple-element.24), kind=kLoop, calls=%fused_computation.172 | loop fusion | bytes 3145728 | tf_op jit(solution)/shard_map/slice | solution.py:306
  64.4 0.9 pad_maximum_fusion.2
  65.4 3.4 %collective-permute-done.1 = bf16[1024,128]{1,0:T(8,128)(2,1)} collective-permute-done((bf16[1024,128]{1,0:T(8,128)(2,1)}, bf16[1024,128]{1,0:T(8,128)(2,1)}, u32[]{:S(2)}, u32[]{:S(2)}) %collective-permute-start.1) | collective-permute-done | bytes 262176 | tf_op jit(solution)/shard_map/ppermute | solution.py:294
  68.8 1.9 %fusion.42 = (f32[]{:T(128)}, bf16[1024,128]{1,0:T(8,128)(2,1)S(1)}) fusion(f32[1024]{0:T(1024)S(1)} %reshape.259, bf16[16,64,128]{2,1,0:T(8,128)(2,1)S(1)} %slice.221, f32[1024,128]{1,0:T(8,128)} %bitcast.258, bf16[1024,128]{1,0:T(8,128)(2,1)} %collective-permute-done.1, bf16[1,128,1024]{1,2,0:T(8,128)(2,1)S(1)} %copy.156), kind=kLoop, calls=%fused_computation.79 | loop fusion | flops 1441791 | bytes 1576964 | tf_op jit(solution)/shard_map/reduce_sum | solution.py:300
  70.9 0.3 convolution_convert_fusion.3
  71.2 0.7 copy.179
  71.9 5.8 %all-to-all-start.3 = ((bf16[16,32,128]{2,1,0:T(8,128)(2,1)}), bf16[16,32,128]{2,1,0:T(8,128)(2,1)S(1)}, u32[]{:S(2)}, u32[]{:S(2)}) async-start(bf16[16,32,128]{2,1,0:T(8,128)(2,1)} %copy.179), calls=%async_computation.3 | async-start | bytes 262144 | tf_op jit(solution)/shard_map/all_to_all | solution.py:251
  77.7 3.5 %fusion.43 = f32[1,32,32,256]{3,0,2,1:T(1,128)S(1)} fusion(bf16[3,3,128,256]{3,2,1,0:T(8,128)(2,1)S(1)} %bitcast.238, bf16[1,32,32,128]{3,2,1,0:T(8,128)(2,1)S(1)} %bitcast.244), kind=kOutput, calls=%fused_computation.83 | convolution fusion | flops 579076096 | bytes 1900544 | tf_op jit(solution)/shard_map/conv_general_dilated | solution.py:25
  81.3 1.1 copy.193
  82.7 0.3 fusion.10
  83.0 0.3 copy-done.7
  83.3 0.3 fusion.9
  83.5 0.3 fusion.8
  83.8 0.3 fusion.7
  84.1 1.5 %all-to-all-done.3 = bf16[16,32,128]{2,1,0:T(8,128)(2,1)S(1)} async-done(((bf16[16,32,128]{2,1,0:T(8,128)(2,1)}), bf16[16,32,128]{2,1,0:T(8,128)(2,1)S(1)}, u32[]{:S(2)}, u32[]{:S(2)}) %all-to-all-start.3) | async-done | bytes 131104 | tf_op jit(solution)/shard_map/all_to_all | solution.py:251
  85.7 0.2 convolution_convert_fusion.5
  86.0 0.4 convolution_convert_fusion
  86.4 0.3 fusion.45
  86.9 0.3 copy-done.6
  87.2 1.5 %fusion.24 = f32[256]{0:T(256)S(1)} fusion(f32[1,32,32,256]{3,0,2,1:T(1,128)S(1)} %copy-done.6, f32[1,32,32,256]{3,0,2,1:T(1,128)S(1)} %copy-done.2, f32[256]{0:T(256)S(1)} %copy-done.16, f32[32,256]{1,0:T(8,128)S(1)} %get-tuple-element.46, f32[32,256]{1,0:T(8,128)S(1)} %get-tuple-element.47, f32[32,256]{1,0:T(8,128)S(1)} %get-tuple-element.48, ...), kind=kLoop, calls=%fused_computation.45 | loop fusion | flops 7601920 | bytes 2230336 | tf_op jit(solution)/shard_map/reduce_sum | solution.py:346
  88.7 0.7 fusion.66.refs_3_
  89.4 1.9 %fusion.17 = (bf16[1024,256]{1,0:T(8,128)(2,1)S(1)}, bf16[1024,256]{1,0:T(8,128)(2,1)S(1)}) fusion(f32[1,32,32,256]{3,2,0,1:T(8,128)S(1)} %copy-done.4, f32[1,32,32,256]{3,2,0,1:T(8,128)S(1)} %copy-done.3, f32[32,256]{1,0:T(8,128)S(1)} %get-tuple-element.46, f32[32,256]{1,0:T(8,128)S(1)} %get-tuple-element.47, f32[32,256]{1,0:T(8,128)S(1)} %get-tuple-element.48, ...), kind=kLoop, calls=%fused_computation.38 | loop fusion | flops 8126464 | bytes 3281920 | tf_op jit(solution)/shard_map/convert_element_type | solution.py:347
  91.3 0.3 fusion.6
  91.6 0.3 fusion.5
  91.9 0.4 copy-done.9
  92.4 0.3 fusion.4
  92.7 0.3 fusion.3
  92.9 0.3 fusion.2
  93.2 42.1 %shard_map.129 = (f32[1152,256]{1,0:T(8,128)S(1)}, f32[2304,128]{1,0:T(8,128)S(1)}, f32[8,128]{1,0:T(8,128)S(1)}) custom-call(f32[1152,256]{1,0:T(8,128)S(1)} %bitcast.240, bf16[1024,256]{1,0:T(8,128)(2,1)S(1)} %get-tuple-element.16.refs_1_, bf16[3,34,32,128]{3,2,1,0:T(8,128)(2,1)S(1)} %pad_maximum_fusion.refs_2_, f32[8,128]{1,0:T(8,128)S(1)} %fusion.66.refs_3_), custom_call_target="tpu_custom_call" | custom-call | tf_op jit(solution)/shard_map/pallas_call | solution.py:200
  135.4 0.5 slice.198
  135.9 0.6 slice_bitcast_fusion.10
  137.1 1.0 copy.261
  138.1 1.0 copy.262
  (103 shorter events, 3.0 us)
Async XLA Ops:
  0.6 54.7 %copy-start = (bf16[9,128,256]{2,1,0:T(8,128)(2,1)S(1)}, bf16[9,128,256]{2,1,0:T(8,128)(2,1)}, u32[]{:S(2)}) copy-start(bf16[9,128,256]{2,1,0:T(8,128)(2,1)} %param.13) | copy-start | bytes 1769476
  0.6 13.6 %copy-start.17 = (s32[16,4]{0,1:T(4,128)S(1)}, s32[16,4]{0,1:T(4,128)}, u32[]{:S(2)}) copy-start(s32[16,4]{0,1:T(4,128)} %param.15) | copy-start | bytes 772
  0.7 13.8 %copy-start.20 = (s32[16,4]{0,1:T(4,128)S(1)}, s32[16,4]{0,1:T(4,128)}, u32[]{:S(2)}) copy-start(s32[16,4]{0,1:T(4,128)} %param.14) | copy-start | bytes 772
  0.7 21.3 %copy-start.19 = (bf16[1,1024]{1,0:T(2,128)(2,1)S(1)}, bf16[1,1024]{1,0:T(2,128)(2,1)}, u32[]{:S(2)}) copy-start(bf16[1,1024]{1,0:T(2,128)(2,1)} %param.18) | copy-start | bytes 6148
  1.8 20.3 %collective-permute-start = (bf16[64,1024]{0,1:T(8,128)(2,1)S(1)}, bf16[64,1024]{0,1:T(8,128)(2,1)S(1)}, u32[]{:S(2)}, u32[]{:S(2)}) collective-permute-start(bf16[64,1024]{0,1:T(8,128)(2,1)S(1)} %bitcast.260), channel_id=1, source_target_pairs={{0,1},{1,0},{2,3},{3,2},{4,5},{5,4},{6,7},{7,6},{8,9},{9,8},{10,11... | collective-permute-start | bytes 393224 | tf_op jit(solution)/shard_map/ppermute | solution.py:257
  15.7 14.1 %all-to-all-start = ((bf16[16,32,128]{2,1,0:T(8,128)(2,1)}), bf16[16,32,128]{2,1,0:T(8,128)(2,1)S(1)}, u32[]{:S(2)}, u32[]{:S(2)}) async-start(bf16[16,32,128]{2,1,0:T(8,128)(2,1)} %copy.158), calls=%async_computation | async-start | bytes 262144 | tf_op jit(solution)/shard_map/all_to_all | solution.py:251
  22.1 0.7 copy-start.21
  30.4 4.6 %copy-start.16 = (f32[256]{0:T(256)S(1)}, f32[256]{0:T(256)}, u32[]{:S(2)}) copy-start(f32[256]{0:T(256)} %param.12) | copy-start | bytes 3076
  35.0 7.2 %copy-start.1 = (f32[1,32,32,256]{3,0,2,1:T(1,128)}, f32[1,32,32,256]{3,0,2,1:T(1,128)S(1)}, u32[]{:S(2)}) copy-start(f32[1,32,32,256]{3,0,2,1:T(1,128)S(1)} %fusion.39) | copy-start | bytes 3145732
  35.3 5.0 %copy-start.15 = (s32[4,3]{1,0:T(4,128)S(1)}, s32[4,3]{1,0:T(4,128)}, u32[]{:S(2)}) copy-start(s32[4,3]{1,0:T(4,128)} %constant.75.clone) | copy-start | bytes 148
  36.8 13.5 %all-to-all-start.2 = ((bf16[16,32,256]{2,1,0:T(8,128)(2,1)}), bf16[16,32,256]{2,1,0:T(8,128)(2,1)S(1)}, u32[]{:S(2)}, u32[]{:S(2)}) async-start(bf16[16,32,256]{2,1,0:T(8,128)(2,1)} %copy.167), calls=%async_computation.2 | async-start | bytes 524288 | tf_op jit(solution)/shard_map/all_to_all | solution.py:251
  50.4 14.9 %all-to-all-start.1 = ((bf16[16,65,128]{2,1,0:T(8,128)(2,1)}), bf16[16,65,128]{2,1,0:T(8,128)(2,1)S(1)}, u32[]{:S(2)}, u32[]{:S(2)}) async-start(bf16[16,65,128]{2,1,0:T(8,128)(2,1)} %copy.159), calls=%async_computation.1 | async-start | bytes 589824 | tf_op jit(solution)/shard_map/all_to_all | solution.py:251
  59.3 5.1 %copy-start.14 = (f32[1,32,32,128]{3,0,2,1:T(1,128)}, f32[1,32,32,128]{3,0,2,1:T(1,128)S(1)}, u32[]{:S(2)}) copy-start(f32[1,32,32,128]{3,0,2,1:T(1,128)S(1)} %fusion) | copy-start | bytes 1572868
  60.1 8.6 %collective-permute-start.1 = (bf16[1024,128]{1,0:T(8,128)(2,1)}, bf16[1024,128]{1,0:T(8,128)(2,1)}, u32[]{:S(2)}, u32[]{:S(2)}) collective-permute-start(bf16[1024,128]{1,0:T(8,128)(2,1)} %convert_element_type.91), channel_id=1, source_target_pairs={{0,1},{1,0},{2,3},{3,2},{4,5},{5,4},{6,7},{7,6},{8,9},{9,8},{10,11... | collective-permute-start | bytes 786440 | tf_op jit(solution)/shard_map/ppermute | solution.py:294
  71.9 13.8 %all-to-all-start.3 = ((bf16[16,32,128]{2,1,0:T(8,128)(2,1)}), bf16[16,32,128]{2,1,0:T(8,128)(2,1)S(1)}, u32[]{:S(2)}, u32[]{:S(2)}) async-start(bf16[16,32,128]{2,1,0:T(8,128)(2,1)} %copy.179), calls=%async_computation.3 | async-start | bytes 262144 | tf_op jit(solution)/shard_map/all_to_all | solution.py:251
  81.3 1.3 copy-start.5
  81.3 1.4 %copy-start.12 = (bf16[32,32,256]{2,1,0:T(8,128)(2,1)S(1)}, bf16[32,32,256]{2,1,0:T(8,128)(2,1)}, u32[]{:S(2)}) copy-start(bf16[32,32,256]{2,1,0:T(8,128)(2,1)} %get-tuple-element.23) | copy-start | bytes 1572868
  81.3 1.9 %copy-start.7 = (bf16[32,32,256]{2,1,0:T(8,128)(2,1)S(1)}, bf16[32,32,256]{2,1,0:T(8,128)(2,1)}, u32[]{:S(2)}) copy-start(bf16[32,32,256]{2,1,0:T(8,128)(2,1)} %get-tuple-element.27) | copy-start | bytes 1572868
  82.4 1.1 copy-start.13
  82.7 1.1 copy-start.11
  85.7 1.2 copy-start.2
  85.7 1.5 %copy-start.6 = (f32[1,32,32,256]{3,0,2,1:T(1,128)S(1)}, f32[1,32,32,256]{3,0,2,1:T(1,128)}, u32[]{:S(2)}) copy-start(f32[1,32,32,256]{3,0,2,1:T(1,128)} %copy-done.5) | copy-start | bytes 3145732
  86.7 2.7 %copy-start.3 = (f32[1,32,32,256]{3,2,0,1:T(8,128)S(1)}, f32[1,32,32,256]{3,2,0,1:T(8,128)}, u32[]{:S(2)}) copy-start(f32[1,32,32,256]{3,2,0,1:T(8,128)} %copy.189) | copy-start | bytes 3145732
  86.7 2.7 %copy-start.4 = (f32[1,32,32,256]{3,2,0,1:T(8,128)S(1)}, f32[1,32,32,256]{3,2,0,1:T(8,128)}, u32[]{:S(2)}) copy-start(f32[1,32,32,256]{3,2,0,1:T(8,128)} %copy.193) | copy-start | bytes 3145732
  86.7 2.7 %copy-start.18 = (pred[1024]{0:T(1024)(128)(4,1)S(1)}, pred[1024]{0:T(1024)(128)(4,1)}, u32[]{:S(2)}) copy-start(pred[1024]{0:T(1024)(128)(4,1)} %broadcast_in_dim.185) | copy-start | bytes 3076
  89.4 2.2 %copy-start.10 = (bf16[32,32,256]{2,1,0:T(8,128)(2,1)S(1)}, bf16[32,32,256]{2,1,0:T(8,128)(2,1)}, u32[]{:S(2)}) copy-start(bf16[32,32,256]{2,1,0:T(8,128)(2,1)} %get-tuple-element.19) | copy-start | bytes 1572868
  91.3 1.0 copy-start.9
  91.6 1.3 copy-start.8
